TPU v7x, 256 devices: a whole 4x4x8 slice. The times are simulated.
256 devices in a mesh: path: 8 (over z_lo, core), shard: 32 (over z_hi, x, y).
Axes of the slice: x: 4, y: 4, z: 8 (z_hi: 2, z_lo: 4; z = z_hi * 4 + z_lo), core: 2. Of those that a mesh axis runs over, the one named last changes fastest.
Arguments:
- tokens: bfloat16 [3072, 2048], P(('path', 'shard')), may hold values from -6 to 6
- routes: int32 [3072, 1], P(('path', 'shard')), may hold values from 0 to 7; in each aligned block of 12 rows (0 to 11, 12 to 23, ...) at most 2 rows name the same one
- cotangent: bfloat16 [3072, 2048], P(('path', 'shard')), may hold values from -6 to 6
- gains: bfloat16 [8, 2, 2048], P('path'), may hold values from 0.099609375 to 1.8984375
- w_in: bfloat16 [8, 2, 2048, 8192], P('path', None, None, 'shard'), may hold values from -0.125 to 0.125
- w_out: bfloat16 [8, 2, 8192, 2048], P('path', None, 'shard'), may hold values from -0.0625 to 0.0625
- partners: int32 [2, 8], replicated, may hold values from 0 to 7, as said below
Outputs:
- delta_in: bfloat16 [8, 2, 2048, 8192], P('path', None, None, 'shard')
- delta_out: bfloat16 [8, 2, 8192, 2048], P('path', None, 'shard')
Inputs may be any that keep to these rules, and one draw needn't show every extreme that they name: `routes`: in each device's block of 12 rows at most 2 rows name one path, and some path gets exactly 2 rows of some block. Each row pairs the paths: partners[l, partners[l, p]] = p and partners[l, p] != p.
All inputs are finite; a program needn't handle non-finite values.
Results may differ from a plain program's by a relative error of at most 0.03.
Values may be sent and summed in bfloat16 or wider, within the bound.
A program may use at most 64 MiB of HBM per device.

v0:
```python
import jax
import jax.numpy as jnp
from jax import lax
from jax.sharding import PartitionSpec as P

SLOTS = 16


def norm_value(v, gain):
    return v * lax.rsqrt(jnp.mean(v * v, axis=-1, keepdims=True) + 1e-05) * gain.astype(jnp.float32)


def norm_pull(h, gain, grad):

    def value(v):
        return norm_value(v, gain)

    return jax.vjp(value, h.astype(jnp.float32))[1](grad)[0]


def gelu_pull(pre, grad):
    return jax.vjp(jax.nn.gelu, pre)[1](grad)[0]


def pair_mean(piece, table):
    paths = table.shape[0]
    pick = (table[:, None] == jnp.arange(paths, dtype=jnp.int32)[None, :]).astype(jnp.float32)
    values = piece.astype(jnp.float32)
    other = jnp.einsum("pq,qrc->prc", pick, values, precision=lax.Precision.HIGHEST)
    return ((values + other) * 0.5).astype(jnp.bfloat16)


def body(tokens, routes, cotangent, gains, w_in, w_out, partners):
    paths = lax.axis_size("path")
    slots = SLOTS
    cap = slots // paths
    width = tokens.shape[1]
    route = routes[:, 0]
    order = jnp.arange(route.shape[0], dtype=jnp.int32)
    same = (route[:, None] == route[None, :]) & (order[None, :] < order[:, None])
    rank = jnp.sum(same.astype(jnp.int32), axis=1)
    target = route * cap + rank
    select = (jnp.arange(slots, dtype=jnp.int32)[:, None] == target[None, :]).astype(jnp.bfloat16)
    packed_x = (
        jnp.dot(select, tokens, preferred_element_type=jnp.float32)
        .astype(jnp.bfloat16)
        .reshape(paths, cap, width)
    )
    packed_dy = (
        jnp.dot(select, cotangent, preferred_element_type=jnp.float32)
        .astype(jnp.bfloat16)
        .reshape(paths, cap, width)
    )
    got_x, got_dy = (
        lax.all_to_all(packed_x, "path", split_axis=0, concat_axis=0, tiled=True),
        lax.all_to_all(packed_dy, "path", split_axis=0, concat_axis=0, tiled=True),
    )
    own_x = got_x.reshape(slots, width)
    own_dy = got_dy.reshape(slots, width)
    full_x, full_dy = (
        lax.all_gather(own_x, "shard", axis=0, tiled=True),
        lax.all_gather(own_dy, "shard", axis=0, tiled=True),
    )
    gain_low = gains[0, 0]
    gain_high = gains[0, 1]
    wi_low = w_in[0, 0]
    wi_high = w_in[0, 1]
    wo_low = w_out[0, 0]
    wo_high = w_out[0, 1]
    hidden = wi_low.shape[1]
    scale = 1.0 / jnp.sqrt(jnp.float32(full_x.shape[0]))
    n1 = norm_value(full_x.astype(jnp.float32), gain_low).astype(jnp.bfloat16)
    a1 = jnp.dot(n1, wi_low, preferred_element_type=jnp.float32)
    u1 = jax.nn.gelu(a1).astype(jnp.bfloat16)
    part_low = jnp.dot(u1, wo_low, preferred_element_type=jnp.float32)
    mixed_own = lax.psum_scatter(
        part_low.astype(jnp.bfloat16), "shard", scatter_dimension=0, tiled=True
    ).astype(jnp.float32)
    h_own = (own_x.astype(jnp.float32) + mixed_own).astype(jnp.bfloat16)
    full_h = lax.all_gather(h_own, "shard", axis=0, tiled=True)
    n2 = norm_value(full_h.astype(jnp.float32), gain_high).astype(jnp.bfloat16)
    a2 = jnp.dot(n2, wi_high, preferred_element_type=jnp.float32)
    u2 = jax.nn.gelu(a2).astype(jnp.bfloat16)
    g_out2 = jnp.dot(u2.T, full_dy, preferred_element_type=jnp.float32)
    du2 = jnp.dot(full_dy, wo_high.T, preferred_element_type=jnp.float32)
    da2 = gelu_pull(a2, du2).astype(jnp.bfloat16)
    g_in2 = jnp.dot(n2.T, da2, preferred_element_type=jnp.float32)
    part_back = jnp.dot(da2, wi_high.T, preferred_element_type=jnp.float32)
    e_in2 = (-g_in2 * scale).astype(jnp.bfloat16).reshape(paths, width // paths, hidden)
    e_out2 = (-g_out2 * scale).astype(jnp.bfloat16).reshape(paths, width // paths, hidden)
    back_own = lax.psum_scatter(
        part_back.astype(jnp.bfloat16), "shard", scatter_dimension=0, tiled=True
    ).astype(jnp.float32)
    dh_own = (own_dy.astype(jnp.float32) + norm_pull(h_own, gain_high, back_own)).astype(
        jnp.bfloat16
    )
    full_dh = lax.all_gather(dh_own, "shard", axis=0, tiled=True)
    g_out1 = jnp.dot(u1.T, full_dh, preferred_element_type=jnp.float32)
    du1 = jnp.dot(full_dh, wo_low.T, preferred_element_type=jnp.float32)
    da1 = gelu_pull(a1, du1).astype(jnp.bfloat16)
    g_in1 = jnp.dot(n1.T, da1, preferred_element_type=jnp.float32)
    e_in1 = (-g_in1 * scale).astype(jnp.bfloat16).reshape(paths, width // paths, hidden)
    e_out1 = (-g_out1 * scale).astype(jnp.bfloat16).reshape(paths, width // paths, hidden)
    avg_in1 = lax.all_to_all(
        pair_mean(
            lax.all_to_all(e_in1, "path", split_axis=0, concat_axis=0, tiled=True), partners[0]
        ),
        "path",
        split_axis=0,
        concat_axis=0,
        tiled=True,
    )
    avg_out1 = lax.all_to_all(
        pair_mean(
            lax.all_to_all(e_out1, "path", split_axis=0, concat_axis=0, tiled=True), partners[0]
        ),
        "path",
        split_axis=0,
        concat_axis=0,
        tiled=True,
    )
    avg_in2 = lax.all_to_all(
        pair_mean(
            lax.all_to_all(e_in2, "path", split_axis=0, concat_axis=0, tiled=True), partners[1]
        ),
        "path",
        split_axis=0,
        concat_axis=0,
        tiled=True,
    )
    avg_out2 = lax.all_to_all(
        pair_mean(
            lax.all_to_all(e_out2, "path", split_axis=0, concat_axis=0, tiled=True), partners[1]
        ),
        "path",
        split_axis=0,
        concat_axis=0,
        tiled=True,
    )
    delta_in = jnp.stack([avg_in1.reshape(width, hidden), avg_in2.reshape(width, hidden)])[None]
    delta_out = jnp.stack([avg_out1.reshape(hidden, width), avg_out2.reshape(hidden, width)])[None]
    return (delta_in, delta_out)


def solution(mesh):
    in_specs = (
        P(("path", "shard"), None),
        P(("path", "shard"), None),
        P(("path", "shard"), None),
        P("path", None, None),
        P("path", None, None, "shard"),
        P("path", None, "shard", None),
        P(),
    )
    out_specs = (P("path", None, None, "shard"), P("path", None, "shard", None))
    return jax.shard_map(body, mesh=mesh, in_specs=in_specs, out_specs=out_specs, check_vma=False)
```

profile of v0, /device:TPU:1, one launch (start us, length us, event | category | flops | bytes accessed | tf_op | source)
XLA Modules:
  0.0 991.5 jit_solution(13657977929646993335)
XLA Ops:
  7.2 0.9 convert_reduce_fusion
  8.1 0.7 multiply_add_fusion.1
  8.8 0.1 convolution_convert_fusion.3
  8.9 0.1 reshape.85
  9.0 12.3 %all_to_all.50 = bf16[8,2,2048]{2,1,0:T(2,128)(2,1)S(1)} all-to-all(bf16[8,2,2048]{2,1,0:T(2,128)(2,1)S(1)} %reshape.85), channel_id=1, replica_groups=mesh['path'=8,'shard'=32] {'path'}, dimensions={0} | all-to-all | bytes 131072 | tf_op jit(solution)/shard_map/all_to_all | solution.py:55
  21.3 0.7 reshape.86
  22.0 0.0 reduce-scatter.3.cloned.1.call-start
  22.0 0.8 slice_convert_fusion
  22.8 90.0 %all-gather.5.cloned.1.call-done = bf16[512,2048]{1,0:T(8,128)(2,1)} async-done(((bf16[16,2048]{1,0:T(8,128)(2,1)}), bf16[512,2048]{1,0:T(8,128)(2,1)}) %all-gather.5.cloned.1.call-update) | async-done | bytes 2097168 | tf_op jit(solution)/shard_map/all_gather | solution.py:61
  112.8 2.2 fusion
  115.1 2.1 fusion.20
  117.2 0.8 copy-done.9
  118.0 2.1 convolution_convert_fusion.1
  120.2 0.0 all-gather.9.cloned.1.call-start
  120.2 200.0 %reduce-scatter.3.cloned.1.call-done = bf16[16,2048]{1,0:T(8,128)(2,1)} async-done(((bf16[512,2048]{1,0:T(8,128)(2,1)}), bf16[16,2048]{1,0:T(8,128)(2,1)}) %reduce-scatter.3.cloned.1.call-update) | async-done | bytes 65552 | tf_op jit(solution)/shard_map/reduce_scatter | solution.py:76
  320.2 1.5 add_convert_fusion
  321.7 0.0 all-gather.7.cloned.1.call-start
  321.8 0.1 convolution_convert_fusion.2
  321.9 0.1 reshape.87
  322.0 33.7 %all_to_all.51 = bf16[8,2,2048]{2,1,0:T(2,128)(2,1)S(1)} all-to-all(bf16[8,2,2048]{2,1,0:T(2,128)(2,1)S(1)} %reshape.87), channel_id=1, replica_groups=mesh['path'=8,'shard'=32] {'path'}, dimensions={0} | all-to-all | bytes 131072 | tf_op jit(solution)/shard_map/all_to_all | solution.py:56
  355.6 0.7 reshape.88
  356.4 75.9 %all-gather.9.cloned.1.call-done = bf16[512,2048]{1,0:T(8,128)(2,1)} async-done(((bf16[16,2048]{1,0:T(8,128)(2,1)}), bf16[512,2048]{1,0:T(8,128)(2,1)}) %all-gather.9.cloned.1.call-update) | async-done | bytes 2097168 | tf_op jit(solution)/shard_map/all_gather | solution.py:80
  432.3 2.2 fusion.3
  434.5 2.0 fusion.15
  436.5 85.4 %all-gather.7.cloned.1.call-done = bf16[512,2048]{1,0:T(8,128)(2,1)} async-done(((bf16[16,2048]{1,0:T(8,128)(2,1)}), bf16[512,2048]{1,0:T(8,128)(2,1)}) %all-gather.7.cloned.1.call-update) | async-done | bytes 2097168 | tf_op jit(solution)/shard_map/all_gather | solution.py:62
  521.9 2.9 fusion.51
  524.8 2.1 convolution_convert_fusion
  526.9 2.5 fusion.13
  529.5 1.3 reshape.92
  530.8 5.8 all-to-all-start.8
  536.6 2.0 fusion.11
  538.6 29.5 %all-to-all-done.8 = bf16[8,256,256]{2,1,0:T(8,128)(2,1)S(1)} async-done(((bf16[8,256,256]{2,1,0:T(8,128)(2,1)}), bf16[8,256,256]{2,1,0:T(8,128)(2,1)S(1)}, u32[]{:S(2)}, u32[]{:S(2)}) %all-to-all-start.8) | async-done | bytes 1048608 | tf_op jit(solution)/shard_map/all_to_all | solution.py:133
  568.1 4.4 all-to-all-start.4
  572.5 156.6 %reduce-scatter.5.cloned.1.call-done = bf16[16,2048]{1,0:T(8,128)(2,1)} async-done(((bf16[512,2048]{1,0:T(8,128)(2,1)}), bf16[16,2048]{1,0:T(8,128)(2,1)}) %reduce-scatter.5.cloned.1.call-update) | async-done | bytes 65552 | tf_op jit(solution)/shard_map/reduce_scatter | solution.py:91
  729.2 1.0 fusion.71
  730.2 1.6 fusion.74
  731.8 1.2 multiply_convert_fusion
  733.0 1.2 copy.42
  734.3 32.9 %all-to-all-start.9 = ((bf16[8,256,256]{2,1,0:T(8,128)(2,1)}), bf16[8,256,256]{2,1,0:T(8,128)(2,1)S(1)}, u32[]{:S(2)}, u32[]{:S(2)}) async-start(bf16[8,256,256]{2,1,0:T(8,128)(2,1)} %copy.42), calls=%async_computation.11 | async-start | bytes 2097152 | tf_op jit(solution)/shard_map/all_to_all | solution.py:131
  767.2 1.2 multiply_convert_fusion.2
  768.4 1.2 copy.36
  769.6 24.2 %all-to-all-done.9 = bf16[8,256,256]{2,1,0:T(8,128)(2,1)S(1)} async-done(((bf16[8,256,256]{2,1,0:T(8,128)(2,1)}), bf16[8,256,256]{2,1,0:T(8,128)(2,1)S(1)}, u32[]{:S(2)}, u32[]{:S(2)}) %all-to-all-start.9) | async-done | bytes 1048608 | tf_op jit(solution)/shard_map/all_to_all | solution.py:131
  793.8 4.3 all-to-all-start.5
  798.1 55.1 %all-gather.11.cloned.1.call-done = bf16[512,2048]{1,0:T(8,128)(2,1)} async-done(((bf16[16,2048]{1,0:T(8,128)(2,1)}), bf16[512,2048]{1,0:T(8,128)(2,1)}) %all-gather.11.cloned.1.call-update) | async-done | bytes 2097168 | tf_op jit(solution)/shard_map/all_gather | solution.py:97
  853.2 5.9 fusion.10
  859.2 5.8 all-to-all-start.2
  864.9 3.5 fusion.12
  868.5 2.3 reshape.91
  870.8 19.9 %all-to-all-done.2 = bf16[8,256,256]{2,1,0:T(8,128)(2,1)S(1)} async-done(((bf16[8,256,256]{2,1,0:T(8,128)(2,1)}), bf16[8,256,256]{2,1,0:T(8,128)(2,1)S(1)}, u32[]{:S(2)}, u32[]{:S(2)}) %all-to-all-start.2) | async-done | bytes 1048608 | tf_op jit(solution)/shard_map/all_to_all | solution.py:106
  890.7 5.0 all-to-all-start.6
  895.7 1.2 multiply_convert_fusion.3
  896.9 1.2 copy.33
  898.1 23.4 %all-to-all-done.6 = bf16[8,256,256]{2,1,0:T(8,128)(2,1)} async-done(((bf16[8,256,256]{2,1,0:T(8,128)(2,1)}), bf16[8,256,256]{2,1,0:T(8,128)(2,1)}, u32[]{:S(2)}, u32[]{:S(2)}) %all-to-all-start.6) | async-done | bytes 1048608 | tf_op jit(solution)/shard_map/all_to_all | solution.py:115
  921.5 4.3 all-to-all-start.3
  925.9 2.8 multiply_convert_fusion.1
  928.7 1.2 copy.39
  929.9 21.7 %all-to-all-done.3 = bf16[8,256,256]{2,1,0:T(8,128)(2,1)S(1)} async-done(((bf16[8,256,256]{2,1,0:T(8,128)(2,1)}), bf16[8,256,256]{2,1,0:T(8,128)(2,1)S(1)}, u32[]{:S(2)}, u32[]{:S(2)}) %all-to-all-start.3) | async-done | bytes 1048608 | tf_op jit(solution)/shard_map/all_to_all | solution.py:104
  951.6 1.0 copy-done.1
  952.6 4.3 all-to-all-start.7
  956.9 1.3 stack_reshape.15
  958.2 2.7 maximum_bitcast_fusion
  961.0 21.7 %all-to-all-done.7 = bf16[8,256,256]{2,1,0:T(8,128)(2,1)S(1)} async-done(((bf16[8,256,256]{2,1,0:T(8,128)(2,1)}), bf16[8,256,256]{2,1,0:T(8,128)(2,1)S(1)}, u32[]{:S(2)}, u32[]{:S(2)}) %all-to-all-start.7) | async-done | bytes 1048608 | tf_op jit(solution)/shard_map/all_to_all | solution.py:113
  982.7 0.5 stack_reshape.14
  983.2 1.5 maximum_bitcast_fusion.1
  (43 shorter events, 0.3 us)
Async XLA Ops:
  7.2 1.6 copy-start
  7.2 105.6 %all-gather.5.cloned.1.call-start = ((), (), s32[]{:S(2)}) async-start(), calls=%async_computation.12 | async-start | bytes 2162688 | tf_op jit(solution)/shard_map/all_gather | solution.py:61
  22.0 298.2 %reduce-scatter.3.cloned.1.call-start = ((), (), s32[]{:S(2)}) async-start(), calls=%async_computation.14 | async-start | bytes 2162688 | tf_op jit(solution)/shard_map/reduce_scatter | solution.py:76
  112.8 2.2 copy-start.3
  115.0 3.0 copy-start.8
  117.2 0.8 copy-start.9
  118.0 202.2 %copy-start.6 = (bf16[16,2048]{1,0:T(8,128)(2,1)S(1)}, bf16[16,2048]{1,0:T(8,128)(2,1)}, u32[]{:S(2)}) copy-start(bf16[16,2048]{1,0:T(8,128)(2,1)} %reshape.86) | copy-start | bytes 196612
  120.1 201.6 %copy-start.12 = (bf16[12,2048]{1,0:T(8,128)(2,1)S(1)}, bf16[12,2048]{1,0:T(8,128)(2,1)}, u32[]{:S(2)}) copy-start(bf16[12,2048]{1,0:T(8,128)(2,1)} %param.9) | copy-start | bytes 147460
  120.2 312.1 %all-gather.9.cloned.1.call-start = ((), (), s32[]{:S(2)}) async-start(), calls=%async_computation.15 | async-start | bytes 2162688 | tf_op jit(solution)/shard_map/all_gather | solution.py:80
  321.7 200.2 %all-gather.7.cloned.1.call-start = ((), (), s32[]{:S(2)}) async-start(), calls=%async_computation.13 | async-start | bytes 2162688 | tf_op jit(solution)/shard_map/all_gather | solution.py:62
  356.3 372.9 %reduce-scatter.5.cloned.1.call-start = ((), (), s32[]{:S(2)}) async-start(), calls=%async_computation.16 | async-start | bytes 2162688 | tf_op jit(solution)/shard_map/reduce_scatter | solution.py:91
  432.3 2.2 copy-start.4
  436.5 88.3 %copy-start.14 = (f32[512,256]{1,0:T(8,128)}, f32[512,256]{1,0:T(8,128)S(1)}, u32[]{:S(2)}) copy-start(f32[512,256]{1,0:T(8,128)S(1)} %fusion.15) | copy-start | bytes 1572868
  521.9 2.9 copy-start.11
  530.8 37.4 %all-to-all-start.8 = ((bf16[8,256,256]{2,1,0:T(8,128)(2,1)}), bf16[8,256,256]{2,1,0:T(8,128)(2,1)S(1)}, u32[]{:S(2)}, u32[]{:S(2)}) async-start(bf16[8,256,256]{2,1,0:T(8,128)(2,1)} %reshape.92), calls=%async_computation.10 | async-start | bytes 2097152 | tf_op jit(solution)/shard_map/all_to_all | solution.py:133
  538.6 190.6 %copy-start.5 = (bf16[16,2048]{1,0:T(8,128)(2,1)S(1)}, bf16[16,2048]{1,0:T(8,128)(2,1)}, u32[]{:S(2)}) copy-start(bf16[16,2048]{1,0:T(8,128)(2,1)} %add_convert_fusion) | copy-start | bytes 196612
  538.6 191.6 %copy-start.7 = (bf16[16,2048]{1,0:T(8,128)(2,1)S(1)}, bf16[16,2048]{1,0:T(8,128)(2,1)}, u32[]{:S(2)}) copy-start(bf16[16,2048]{1,0:T(8,128)(2,1)} %reshape.88) | copy-start | bytes 196612
  538.6 193.2 %copy-start.13 = (s32[2,8]{1,0:T(2,128)S(1)}, s32[2,8]{1,0:T(2,128)}, u32[]{:S(2)}) copy-start(s32[2,8]{1,0:T(2,128)} %param.13) | copy-start | bytes 196
  568.1 166.1 %all-to-all-start.4 = ((bf16[8,256,256]{2,1,0:T(8,128)(2,1)}), bf16[8,256,256]{2,1,0:T(8,128)(2,1)S(1)}, u32[]{:S(2)}, u32[]{:S(2)}) async-start(bf16[8,256,256]{2,1,0:T(8,128)(2,1)} %bitcast.56), calls=%async_computation.6 | async-start | bytes 2097152 | tf_op jit(solution)/shard_map/all_to_all | solution.py:124
  572.5 280.7 %all-gather.11.cloned.1.call-start = ((), (), s32[]{:S(2)}) async-start(), calls=%async_computation.17 | async-start | bytes 2162688 | tf_op jit(solution)/shard_map/all_gather | solution.py:97
  734.3 59.5 %all-to-all-start.9 = ((bf16[8,256,256]{2,1,0:T(8,128)(2,1)}), bf16[8,256,256]{2,1,0:T(8,128)(2,1)S(1)}, u32[]{:S(2)}, u32[]{:S(2)}) async-start(bf16[8,256,256]{2,1,0:T(8,128)(2,1)} %copy.42), calls=%async_computation.11 | async-start | bytes 2097152 | tf_op jit(solution)/shard_map/all_to_all | solution.py:131
  768.4 84.8 %copy-start.10 = (f32[512,256]{1,0:T(8,128)S(1)}, f32[512,256]{1,0:T(8,128)}, u32[]{:S(2)}) copy-start(f32[512,256]{1,0:T(8,128)} %copy-done.9) | copy-start | bytes 1572868
  793.8 65.3 %all-to-all-start.5 = ((bf16[8,256,256]{2,1,0:T(8,128)(2,1)}), bf16[8,256,256]{2,1,0:T(8,128)(2,1)S(1)}, u32[]{:S(2)}, u32[]{:S(2)}) async-start(bf16[8,256,256]{2,1,0:T(8,128)(2,1)} %copy.36), calls=%async_computation.7 | async-start | bytes 2097152 | tf_op jit(solution)/shard_map/all_to_all | solution.py:122
  859.2 31.5 %all-to-all-start.2 = ((bf16[8,256,256]{2,1,0:T(8,128)(2,1)}), bf16[8,256,256]{2,1,0:T(8,128)(2,1)S(1)}, u32[]{:S(2)}, u32[]{:S(2)}) async-start(bf16[8,256,256]{2,1,0:T(8,128)(2,1)} %bitcast.57), calls=%async_computation.4 | async-start | bytes 2097152 | tf_op jit(solution)/shard_map/all_to_all | solution.py:106
  890.7 30.8 %all-to-all-start.6 = ((bf16[8,256,256]{2,1,0:T(8,128)(2,1)}), bf16[8,256,256]{2,1,0:T(8,128)(2,1)}, u32[]{:S(2)}, u32[]{:S(2)}) async-start(bf16[8,256,256]{2,1,0:T(8,128)(2,1)} %reshape.91), calls=%async_computation.8 | async-start | bytes 2097152 | tf_op jit(solution)/shard_map/all_to_all | solution.py:115
  921.5 30.1 %all-to-all-start.3 = ((bf16[8,256,256]{2,1,0:T(8,128)(2,1)}), bf16[8,256,256]{2,1,0:T(8,128)(2,1)S(1)}, u32[]{:S(2)}, u32[]{:S(2)}) async-start(bf16[8,256,256]{2,1,0:T(8,128)(2,1)} %copy.33), calls=%async_computation.5 | async-start | bytes 2097152 | tf_op jit(solution)/shard_map/all_to_all | solution.py:104
  951.6 1.0 copy-start.1
  952.6 30.1 %all-to-all-start.7 = ((bf16[8,256,256]{2,1,0:T(8,128)(2,1)}), bf16[8,256,256]{2,1,0:T(8,128)(2,1)S(1)}, u32[]{:S(2)}, u32[]{:S(2)}) async-start(bf16[8,256,256]{2,1,0:T(8,128)(2,1)} %copy.39), calls=%async_computation.9 | async-start | bytes 2097152 | tf_op jit(solution)/shard_map/all_to_all | solution.py:113
  961.0 22.2 %copy-start.2 = (bf16[1,256,2048]{2,1,0:T(8,128)(2,1)S(1)}, bf16[1,256,2048]{2,1,0:T(8,128)(2,1)}, u32[]{:S(2)}) copy-start(bf16[1,256,2048]{2,1,0:T(8,128)(2,1)} %stack_reshape.15) | copy-start | bytes 3145732
Sparse Core Ops, SparseCore 0:
  22.1 90.6 all-gather.4
  120.3 199.8 reduce-scatter.2
  324.3 107.9 all-gather.8
  436.2 85.6 all-gather.6
  527.0 202.0 reduce-scatter.4
  732.5 120.6 all-gather.10
where the time goes:
time: 993 us; the launch traced here: 992 us
  waiting for transfers between devices  804 us (81%)
  starting transfers between devices  67.1 us (7%)
  blocking collectives  45.9 us (5%)
  matrix products  32.1 us (3%)
  other arithmetic  15.1 us (2%)
  between operations  14.3 us (1%)
  local copies, waits for them, and re-layouts  13.5 us (1%)
    reduce_scatter x1, waiting for transfers between devices, body(): lax.psum_scatter(part_low.astype(jnp.bfloat16), 'shard', scatter_dimensio...  200 us
    reduce_scatter x1, waiting for transfers between devices, body(): lax.psum_scatter(part_back.astype(jnp.bfloat16), 'shard', scatter_dimensi...  157 us
    all_gather x1, waiting for transfers between devices, body(): lax.all_gather(own_x, 'shard', axis=0, tiled=True)  90 us
    all_gather x1, waiting for transfers between devices, body(): lax.all_gather(own_dy, 'shard', axis=0, tiled=True)  85.4 us
    all_gather x1, waiting for transfers between devices, body(): full_h = lax.all_gather(h_own, 'shard', axis=0, tiled=True)  75.9 us
    all_gather x1, waiting for transfers between devices, body(): full_dh = lax.all_gather(dh_own, 'shard', axis=0, tiled=True)  55.1 us
    all_to_all x1, blocking collectives, body(): lax.all_to_all(packed_dy, 'path', split_axis=0, concat_axis=0, tiled=True)  33.7 us
    all_to_all x1, starting transfers between devices, body(): lax.all_to_all(pair_mean(lax.all_to_all(e_out2, 'path', split_axis=0, con...  32.9 us
  transfers between devices with their start and end apart: 14, of which 12 were waited for; matrix products, arithmetic and copies ran while one was open for 4% of the time, Pallas kernels for 0%

commit v1 on v0

--- a/solution.py
+++ b/solution.py
@@ -1,9 +1,290 @@
+import functools
+
 import jax
 import jax.numpy as jnp
 from jax import lax
+from jax.experimental import pallas as pl
+from jax.experimental.pallas import tpu as pltpu
 from jax.sharding import PartitionSpec as P
 
 SLOTS = 16
+MESH = pl.DeviceIdType.MESH
+BF = jnp.bfloat16
+F32 = jnp.float32
+HALF = 1024
+QUARTER = 512
+
+
+class Wires:
+    def __init__(self, send, recv):
+        self.send, self.recv, self.made = send, recv, []
+        shard = lax.axis_index("shard")
+        self.zh = shard // 16
+        self.x = lax.rem(shard // 4, 4)
+        self.y = lax.rem(shard, 4)
+
+    def shard(self, zh, x, y):
+        return {"shard": zh * 16 + x * 4 + y}
+
+    def xs(self, step):
+        return lax.rem(self.x + step + 4, 4)
+
+    def ys(self, step):
+        return lax.rem(self.y + step + 4, 4)
+
+    def pos(self, axis, step):
+        return self.xs(step) if axis == "x" else self.ys(step)
+
+    def beside(self, axis, step):
+        if axis == "x":
+            return self.shard(self.zh, self.xs(step), self.y)
+        return self.shard(self.zh, self.x, self.ys(step))
+
+    def across(self):
+        return self.shard(1 - self.zh, self.x, self.y)
+
+    def push(self, src, dst, to):
+        k = len(self.made)
+        copy = pltpu.make_async_remote_copy(
+            src_ref=src,
+            dst_ref=dst,
+            send_sem=self.send.at[k],
+            recv_sem=self.recv.at[k],
+            device_id=to,
+            device_id_type=MESH,
+        )
+        copy.start()
+        self.made.append(copy)
+        return copy
+
+    def drain(self):
+        for copy in self.made:
+            copy.wait_send()
+
+    def greet(self):
+        barrier = pltpu.get_barrier_semaphore()
+        for to in (
+            self.beside("x", 1),
+            self.beside("x", -1),
+            self.beside("y", 1),
+            self.beside("y", -1),
+            self.across(),
+        ):
+            pl.semaphore_signal(barrier, inc=1, device_id=to, device_id_type=MESH)
+        pl.semaphore_wait(barrier, 5)
+
+
+def run(*tasks):
+    tasks = list(tasks)
+    while tasks:
+        for task in list(tasks):
+            try:
+                next(task)
+            except StopIteration:
+                tasks.remove(task)
+
+
+def ring_gather(w, axis, view, low, size):
+    here, left, right = w.pos(axis, 0), w.pos(axis, -1), w.pos(axis, 1)
+    own = view(here, low, size)
+    go_right = w.push(own, own, w.beside(axis, 1))
+    go_left = w.push(own, own, w.beside(axis, -1))
+    yield
+    go_right.wait_recv()
+    part = view(left, low, size // 2)
+    on_right = w.push(part, part, w.beside(axis, 1))
+    yield
+    go_left.wait_recv()
+    part = view(right, low + size // 2, size // 2)
+    on_left = w.push(part, part, w.beside(axis, -1))
+    yield
+    on_right.wait_recv()
+    on_left.wait_recv()
+
+
+def gather(w, full):
+    own = full.at[w.zh, w.x, w.y]
+    over = w.push(own, own, w.across())
+
+    def half(plane, first, second, low, wait):
+        if wait:
+            yield
+            over.wait_recv()
+
+        def line(i, start, size):
+            cols = pl.ds(start, size)
+            if first == "x":
+                return full.at[plane, i, w.y, :, cols]
+            return full.at[plane, w.x, i, :, cols]
+
+        def sheet(i, start, size):
+            cols = pl.ds(start, size)
+            if second == "x":
+                return full.at[plane, i, :, :, cols]
+            return full.at[plane, :, i, :, cols]
+
+        yield from ring_gather(w, first, line, low, HALF)
+        yield from ring_gather(w, second, sheet, low, HALF)
+
+    waited = []
+
+    def other(first, second, low):
+        yield
+        if not waited:
+            over.wait_recv()
+            waited.append(True)
+        yield from half(1 - w.zh, first, second, low, False)
+
+    return [
+        half(w.zh, "x", "y", 0, False),
+        half(w.zh, "y", "x", HALF, False),
+        other("x", "y", 0),
+        other("y", "x", HALF),
+    ]
+
+
+def ring_reduce(w, axis, view, low, bufs, out):
+    from_left, from_right, in_r_lo, in_r_hi, in_l_lo, in_l_hi, tmp_r, tmp_l = bufs
+    q = QUARTER
+    here, left, right, far = (w.pos(axis, s) for s in (0, -1, 1, 2))
+    to_right, to_left = w.beside(axis, 1), w.beside(axis, -1)
+    a = w.push(view(far, low, q), from_left, to_right)
+    b = w.push(view(far, low + q, q), from_right, to_left)
+    c = w.push(view(right, low + q, q), in_r_hi, to_right)
+    d = w.push(view(left, low, q), in_l_lo, to_left)
+    yield
+    a.wait_recv()
+    tmp_r[...] = (view(right, low, q)[...].astype(F32) + from_left[...].astype(F32)).astype(BF)
+    e = w.push(tmp_r, in_r_lo, to_right)
+    yield
+    b.wait_recv()
+    tmp_l[...] = (view(left, low + q, q)[...].astype(F32) + from_right[...].astype(F32)).astype(BF)
+    f = w.push(tmp_l, in_l_hi, to_left)
+    yield
+    c.wait_recv()
+    f.wait_recv()
+    hi = (
+        view(here, low + q, q)[...].astype(F32)
+        + in_r_hi[...].astype(F32)
+        + in_l_hi[...].astype(F32)
+    )
+    out(1, hi)
+    yield
+    d.wait_recv()
+    e.wait_recv()
+    lo = view(here, low, q)[...].astype(F32) + in_r_lo[...].astype(F32) + in_l_lo[...].astype(F32)
+    out(0, lo)
+
+
+def reduce(w, part, big, small, mid, far, near, total):
+    over = {}
+
+    def half(k, plane, mine, first, second, low):
+        def sheet(i, start, size):
+            cols = pl.ds(start, size)
+            if first == "x":
+                return part.at[plane, i, :, :, cols]
+            return part.at[plane, :, i, :, cols]
+
+        def keep(which, value):
+            mid[k, :, :, pl.ds(which * QUARTER, QUARTER)] = value.astype(BF)
+
+        def line(i, start, size):
+            return mid.at[k, i, :, pl.ds(start, size)]
+
+        def last(which, value):
+            cols = pl.ds(low + which * QUARTER, QUARTER)
+            if mine:
+                total[:, cols] = value
+            else:
+                far[:, cols] = value.astype(BF)
+
+        yield from ring_reduce(w, first, sheet, low, [big.at[k, n] for n in range(8)], keep)
+        yield from ring_reduce(w, second, line, 0, [small.at[k, n] for n in range(8)], last)
+        if not mine:
+            cols = pl.ds(low, HALF)
+            over[low] = w.push(far.at[:, cols], near.at[:, cols], w.across())
+
+    def finish():
+        for low in (0, HALF):
+            over[low].wait_recv()
+            cols = pl.ds(low, HALF)
+            total[:, cols] = total[:, cols] + near[:, cols].astype(F32)
+
+    tasks = [
+        half(0, 1 - w.zh, False, "x", "y", 0),
+        half(1, 1 - w.zh, False, "y", "x", HALF),
+        half(2, w.zh, True, "x", "y", 0),
+        half(3, w.zh, True, "y", "x", HALF),
+    ]
+    return tasks, finish
+
+
+def reduce_scratch():
+    return [
+        pltpu.VMEM((4, 8, 4, SLOTS, QUARTER), BF),
+        pltpu.VMEM((4, 8, SLOTS, QUARTER), BF),
+        pltpu.VMEM((4, 4, SLOTS, HALF), BF),
+        pltpu.VMEM((SLOTS, 2 * HALF), BF),
+        pltpu.VMEM((SLOTS, 2 * HALF), BF),
+    ]
+
+
+def gather_kernel(count, *refs):
+    owns, fulls, send, recv = refs[:count], refs[count : 2 * count], refs[-2], refs[-1]
+    w = Wires(send, recv)
+    for own, full in zip(owns, fulls):
+        full[w.zh, w.x, w.y] = own[...]
+    w.greet()
+    tasks = []
+    for full in fulls:
+        tasks += gather(w, full)
+    run(*tasks)
+    w.drain()
+
+
+def reduce_kernel(part, total, big, small, mid, far, near, send, recv):
+    w = Wires(send, recv)
+    w.greet()
+    tasks, finish = reduce(w, part, big, small, mid, far, near, total)
+    run(*tasks)
+    finish()
+    w.drain()
+
+
+def vmem():
+    return pl.BlockSpec(memory_space=pltpu.VMEM)
+
+
+def gather_call(number, *owns):
+    count = len(owns)
+    width = owns[0].shape[1]
+    got = pl.pallas_call(
+        functools.partial(gather_kernel, count),
+        out_shape=[jax.ShapeDtypeStruct((2, 4, 4, SLOTS, width), BF)] * count,
+        in_specs=[vmem()] * count,
+        out_specs=[vmem()] * count,
+        scratch_shapes=[pltpu.SemaphoreType.DMA((33 * count,)), pltpu.SemaphoreType.DMA((33 * count,))],
+        compiler_params=pltpu.CompilerParams(
+            collective_id=number, has_side_effects=True, vmem_limit_bytes=40 << 20
+        ),
+    )(*owns)
+    return [full.reshape(512, width) for full in got]
+
+
+def reduce_call(number, part):
+    width = part.shape[1]
+    return pl.pallas_call(
+        reduce_kernel,
+        out_shape=jax.ShapeDtypeStruct((SLOTS, width), F32),
+        in_specs=[vmem()],
+        out_specs=vmem(),
+        scratch_shapes=reduce_scratch()
+        + [pltpu.SemaphoreType.DMA((50,)), pltpu.SemaphoreType.DMA((50,))],
+        compiler_params=pltpu.CompilerParams(
+            collective_id=number, has_side_effects=True, vmem_limit_bytes=40 << 20
+        ),
+    )(part.reshape(2, 4, 4, SLOTS, width))
 
 
 def norm_value(v, gain):
@@ -57,28 +338,22 @@
     )
     own_x = got_x.reshape(slots, width)
     own_dy = got_dy.reshape(slots, width)
-    full_x, full_dy = (
-        lax.all_gather(own_x, "shard", axis=0, tiled=True),
-        lax.all_gather(own_dy, "shard", axis=0, tiled=True),
-    )
-    gain_low = gains[0, 0]
+    own_n1 = norm_value(own_x.astype(jnp.float32), gains[0, 0]).astype(jnp.bfloat16)
+    n1, full_dy = gather_call(0, own_n1, own_dy)
     gain_high = gains[0, 1]
     wi_low = w_in[0, 0]
     wi_high = w_in[0, 1]
     wo_low = w_out[0, 0]
     wo_high = w_out[0, 1]
     hidden = wi_low.shape[1]
-    scale = 1.0 / jnp.sqrt(jnp.float32(full_x.shape[0]))
-    n1 = norm_value(full_x.astype(jnp.float32), gain_low).astype(jnp.bfloat16)
+    scale = 1.0 / jnp.sqrt(jnp.float32(n1.shape[0]))
     a1 = jnp.dot(n1, wi_low, preferred_element_type=jnp.float32)
     u1 = jax.nn.gelu(a1).astype(jnp.bfloat16)
     part_low = jnp.dot(u1, wo_low, preferred_element_type=jnp.float32)
-    mixed_own = lax.psum_scatter(
-        part_low.astype(jnp.bfloat16), "shard", scatter_dimension=0, tiled=True
-    ).astype(jnp.float32)
+    mixed_own = reduce_call(1, part_low.astype(jnp.bfloat16))
     h_own = (own_x.astype(jnp.float32) + mixed_own).astype(jnp.bfloat16)
-    full_h = lax.all_gather(h_own, "shard", axis=0, tiled=True)
-    n2 = norm_value(full_h.astype(jnp.float32), gain_high).astype(jnp.bfloat16)
+    own_n2 = norm_value(h_own.astype(jnp.float32), gain_high).astype(jnp.bfloat16)
+    (n2,) = gather_call(2, own_n2)
     a2 = jnp.dot(n2, wi_high, preferred_element_type=jnp.float32)
     u2 = jax.nn.gelu(a2).astype(jnp.bfloat16)
     g_out2 = jnp.dot(u2.T, full_dy, preferred_element_type=jnp.float32)
@@ -88,13 +363,11 @@
     part_back = jnp.dot(da2, wi_high.T, preferred_element_type=jnp.float32)
     e_in2 = (-g_in2 * scale).astype(jnp.bfloat16).reshape(paths, width // paths, hidden)
     e_out2 = (-g_out2 * scale).astype(jnp.bfloat16).reshape(paths, width // paths, hidden)
-    back_own = lax.psum_scatter(
-        part_back.astype(jnp.bfloat16), "shard", scatter_dimension=0, tiled=True
-    ).astype(jnp.float32)
+    back_own = reduce_call(3, part_back.astype(jnp.bfloat16))
     dh_own = (own_dy.astype(jnp.float32) + norm_pull(h_own, gain_high, back_own)).astype(
         jnp.bfloat16
     )
-    full_dh = lax.all_gather(dh_own, "shard", axis=0, tiled=True)
+    (full_dh,) = gather_call(4, dh_own)
     g_out1 = jnp.dot(u1.T, full_dh, preferred_element_type=jnp.float32)
     du1 = jnp.dot(full_dh, wo_low.T, preferred_element_type=jnp.float32)
     da1 = gelu_pull(a1, du1).astype(jnp.bfloat16)

time: 993 us -> 413 us (0.42)
  waiting for transfers between devices: 804 us -> 159 us
  Pallas kernels: 0 us -> 133 us
  blocking collectives: 45.9 us -> 0 us
  between operations: 14.3 us -> 0.9 us
    reduce_scatter x2 -> x0, waiting for transfers between devices: 357 us -> none  [the longest x1 200 us: body(): lax.psum_scatter(part_low.astype(jnp.bfloat16), 'shard', scatter_dimensio...]
    all_gather x4 -> x0, waiting for transfers between devices: 306 us -> none  [the longest x1 90 us: body(): lax.all_gather(own_x, 'shard', axis=0, tiled=True)]
    pallas_call x0 -> x5, Pallas kernels: none -> 133 us  [the longest x3 85.1 us: gather_call(): pl.pallas_call(functools.partial(gather_kernel, count), out_shape=[jax.Sh...]
    all_to_all x2 -> x0, blocking collectives: 45.9 us -> none  [the longest x1 33.7 us: body(): lax.all_to_all(packed_dy, 'path', split_axis=0, concat_axis=0, tiled=True)]
    all_to_all x1, starting transfers between devices: 32.9 us -> 4.33 us  [body(): lax.all_to_all(pair_mean(lax.all_to_all(e_out2, 'path', split_axis=0, con...]
    all_to_all x1, waiting for transfers between devices: 0.01 us -> 21.8 us  [body(): lax.all_to_all(pair_mean(lax.all_to_all(e_in2, 'path', split_axis=0, conc...]
    all_to_all x0 -> x2, starting transfers between devices: none -> 11.5 us  [the longest x1 7.4 us: body(): lax.all_to_all(packed_x, 'path', split_axis=0, concat_axis=0, tiled=True)]
  transfers between devices with their start and end apart: 14 -> 10, of which waited for: 12 -> 9; matrix products, arithmetic and copies ran while one was open for 4% -> 9% of each run, Pallas kernels for 0% -> 11%
where the time goes in v1:
time: 413 us; the launch traced here: 412 us
  waiting for transfers between devices  159 us (38%)
  Pallas kernels  133 us (32%)
  starting transfers between devices  67.2 us (16%)
  matrix products  30.5 us (7%)
  local copies, waits for them, and re-layouts  14.7 us (4%)
  other arithmetic  7.33 us (2%)
    pallas_call x3, Pallas kernels, gather_call(): pl.pallas_call(functools.partial(gather_kernel, count), out_shape=[jax.Sh...  85.1 us
    pallas_call x2, Pallas kernels, reduce_call(): pl.pallas_call(reduce_kernel, out_shape=jax.ShapeDtypeStruct((SLOTS, widt...  47.6 us
    all_to_all x1, waiting for transfers between devices, body(): lax.all_to_all(e_out1, 'path', split_axis=0, concat_axis=0, tiled=True)  23.3 us
    all_to_all x1, waiting for transfers between devices, body(): lax.all_to_all(pair_mean(lax.all_to_all(e_in1, 'path', split_axis=0, conc...  21.8 us
    all_to_all x1, waiting for transfers between devices, body(): lax.all_to_all(pair_mean(lax.all_to_all(e_in2, 'path', split_axis=0, conc...  21.8 us
    all_to_all x1, waiting for transfers between devices, body(): lax.all_to_all(pair_mean(lax.all_to_all(e_out2, 'path', split_axis=0, con...  21.8 us
    all_to_all x1, waiting for transfers between devices, body(): lax.all_to_all(pair_mean(lax.all_to_all(e_out1, 'path', split_axis=0, con...  21.7 us
    all_to_all x1, waiting for transfers between devices, body(): lax.all_to_all(e_in1, 'path', split_axis=0, concat_axis=0, tiled=True)  20.7 us
  transfers between devices with their start and end apart: 10, of which 9 were waited for; matrix products, arithmetic and copies ran while one was open for 9% of the time, Pallas kernels for 11%

profile of v1, /device:TPU:1, one launch (start us, length us, event | category | flops | bytes accessed | tf_op | source)
XLA Modules:
  0.0 412.2 jit_solution(15333397864522223539)
XLA Ops:
  0.6 0.9 convert_reduce_fusion
  1.6 0.7 multiply_add_fusion.1
  2.2 0.1 convolution_convert_fusion.3
  2.4 0.7 reshape.104
  3.1 7.4 %all-to-all-start = ((bf16[8,2,2048]{2,1,0:T(2,128)(2,1)}), bf16[8,2,2048]{2,1,0:T(2,128)(2,1)S(1)}, u32[]{:S(2)}, u32[]{:S(2)}) async-start(bf16[8,2,2048]{2,1,0:T(2,128)(2,1)} %reshape.104), calls=%async_computation | async-start | bytes 131072 | tf_op jit(solution)/shard_map/all_to_all | solution.py:336
  10.5 0.8 slice_convert_fusion
  11.2 1.0 convolution_convert_fusion.2
  12.2 0.7 reshape.105
  12.9 2.6 all-to-all-done
  15.5 4.1 all-to-all-start.1
  19.6 0.2 multiply_reduce_fusion
  19.9 0.1 multiply_convert_fusion.7.refs_0_
  20.0 4.7 %all-to-all-done.1 = bf16[8,2,2048]{2,1,0:T(2,128)(2,1)S(1)} async-done(((bf16[8,2,2048]{2,1,0:T(2,128)(2,1)}), bf16[8,2,2048]{2,1,0:T(2,128)(2,1)S(1)}, u32[]{:S(2)}, u32[]{:S(2)}) %all-to-all-start.1) | async-done | bytes 65568 | tf_op jit(solution)/shard_map/all_to_all | solution.py:337
  24.8 37.5 %shard_map.86 = (bf16[2,4,4,16,2048]{4,3,2,1,0:T(8,128)(2,1)S(1)}, bf16[2,4,4,16,2048]{4,3,2,1,0:T(8,128)(2,1)S(1)}) custom-call(bf16[16,2048]{1,0:T(8,128)(2,1)S(1)} %multiply_convert_fusion.7.refs_0_, bf16[16,2048]{1,0:T(8,128)(2,1)S(1)} %reshape.106.refs_1_), custom_call_target="tpu_custom_call" | custom-call | tf_op jit(solution)/shard_map/pallas_call | solution.py:262
  62.3 2.9 fusion.14
  65.2 0.5 copy-done.6
  65.7 0.8 convolution_convert_fusion.1
  66.5 23.8 %shard_map.87 = f32[16,2048]{1,0:T(8,128)S(1)} custom-call(bf16[2,4,4,16,2048]{4,3,2,1,0:T(8,128)(2,1)S(1)} %bitcast.64), custom_call_target="tpu_custom_call" | custom-call | tf_op jit(solution)/shard_map/pallas_call | solution.py:277
  90.3 0.1 fusion.63
  90.4 0.1 fusion.65.refs_0_
  90.5 24.1 %shard_map.88 = bf16[2,4,4,16,2048]{4,3,2,1,0:T(8,128)(2,1)S(1)} custom-call(bf16[16,2048]{1,0:T(8,128)(2,1)S(1)} %fusion.65.refs_0_), custom_call_target="tpu_custom_call" | custom-call | tf_op jit(solution)/shard_map/pallas_call | solution.py:262
  114.6 0.7 fusion.9
  115.3 0.8 copy-done.12
  116.1 0.8 fusion.7
  116.9 1.3 reshape.116
  118.2 14.1 %all-to-all-start.8 = ((bf16[8,256,256]{2,1,0:T(8,128)(2,1)}), bf16[8,256,256]{2,1,0:T(8,128)(2,1)S(1)}, u32[]{:S(2)}, u32[]{:S(2)}) async-start(bf16[8,256,256]{2,1,0:T(8,128)(2,1)} %reshape.116), calls=%async_computation.8 | async-start | bytes 2097152 | tf_op jit(solution)/shard_map/all_to_all | solution.py:406
  132.3 2.9 fusion.41
  135.2 0.7 copy-done.10
  135.9 1.7 fusion.5
  137.7 20.4 %all-to-all-done.8 = bf16[8,256,256]{2,1,0:T(8,128)(2,1)S(1)} async-done(((bf16[8,256,256]{2,1,0:T(8,128)(2,1)}), bf16[8,256,256]{2,1,0:T(8,128)(2,1)S(1)}, u32[]{:S(2)}, u32[]{:S(2)}) %all-to-all-start.8) | async-done | bytes 1048608 | tf_op jit(solution)/shard_map/all_to_all | solution.py:406
  158.1 5.0 %all-to-all-start.4 = ((bf16[8,256,256]{2,1,0:T(8,128)(2,1)}), bf16[8,256,256]{2,1,0:T(8,128)(2,1)}, u32[]{:S(2)}, u32[]{:S(2)}) async-start(bf16[8,256,256]{2,1,0:T(8,128)(2,1)} %bitcast.76), calls=%async_computation.4 | async-start | bytes 2097152 | tf_op jit(solution)/shard_map/all_to_all | solution.py:397
  163.0 1.7 convolution_convert_fusion
  164.7 23.8 %shard_map.89 = f32[16,2048]{1,0:T(8,128)S(1)} custom-call(bf16[2,4,4,16,2048]{4,3,2,1,0:T(8,128)(2,1)S(1)} %bitcast.65), custom_call_target="tpu_custom_call" | custom-call | tf_op jit(solution)/shard_map/pallas_call | solution.py:277
  188.6 0.1 fusion.66
  188.7 0.1 fusion.62.refs_0_
  188.8 23.6 %shard_map.90 = bf16[2,4,4,16,2048]{4,3,2,1,0:T(8,128)(2,1)S(1)} custom-call(bf16[16,2048]{1,0:T(8,128)(2,1)S(1)} %fusion.62.refs_0_), custom_call_target="tpu_custom_call" | custom-call | tf_op jit(solution)/shard_map/pallas_call | solution.py:262
  212.4 5.5 %fusion.4 = bf16[2048,256]{1,0:T(8,128)(2,1)} fusion(bf16[512,2048]{1,0:T(8,128)(2,1)} %bitcast.71, f32[512,256]{1,0:T(8,128)} %copy-done.7, bf16[512,2048]{1,0:T(8,128)(2,1)S(1)} %bitcast.68, bf16[1,2,256,2048]{3,2,1,0:T(8,128)(2,1)} %param.12), kind=kOutput, calls=%fused_computation.10 | convolution fusion | flops 1077936128 | bytes 6815744 | tf_op jit(solution)/shard_map/dot_general | solution.py:374
  218.0 15.0 %all-to-all-start.2 = ((bf16[8,256,256]{2,1,0:T(8,128)(2,1)}), bf16[8,256,256]{2,1,0:T(8,128)(2,1)}, u32[]{:S(2)}, u32[]{:S(2)}) async-start(bf16[8,256,256]{2,1,0:T(8,128)(2,1)} %bitcast.77), calls=%async_computation.2 | async-start | bytes 2097152 | tf_op jit(solution)/shard_map/all_to_all | solution.py:379
  232.9 2.8 fusion.6
  235.7 2.3 reshape.115
  238.1 20.7 %all-to-all-done.2 = bf16[8,256,256]{2,1,0:T(8,128)(2,1)} async-done(((bf16[8,256,256]{2,1,0:T(8,128)(2,1)}), bf16[8,256,256]{2,1,0:T(8,128)(2,1)}, u32[]{:S(2)}, u32[]{:S(2)}) %all-to-all-start.2) | async-done | bytes 1048608 | tf_op jit(solution)/shard_map/all_to_all | solution.py:379
  258.8 4.3 %all-to-all-start.6 = ((bf16[8,256,256]{2,1,0:T(8,128)(2,1)}), bf16[8,256,256]{2,1,0:T(8,128)(2,1)S(1)}, u32[]{:S(2)}, u32[]{:S(2)}) async-start(bf16[8,256,256]{2,1,0:T(8,128)(2,1)} %reshape.115), calls=%async_computation.6 | async-start | bytes 2097152 | tf_op jit(solution)/shard_map/all_to_all | solution.py:388
  263.1 1.2 multiply_convert_fusion
  264.3 1.2 copy.42
  265.5 23.3 %all-to-all-done.6 = bf16[8,256,256]{2,1,0:T(8,128)(2,1)S(1)} async-done(((bf16[8,256,256]{2,1,0:T(8,128)(2,1)}), bf16[8,256,256]{2,1,0:T(8,128)(2,1)S(1)}, u32[]{:S(2)}, u32[]{:S(2)}) %all-to-all-start.6) | async-done | bytes 1048608 | tf_op jit(solution)/shard_map/all_to_all | solution.py:388
  288.8 4.3 %all-to-all-start.9 = ((bf16[8,256,256]{2,1,0:T(8,128)(2,1)}), bf16[8,256,256]{2,1,0:T(8,128)(2,1)S(1)}, u32[]{:S(2)}, u32[]{:S(2)}) async-start(bf16[8,256,256]{2,1,0:T(8,128)(2,1)} %copy.42), calls=%async_computation.9 | async-start | bytes 2097152 | tf_op jit(solution)/shard_map/all_to_all | solution.py:404
  293.2 2.8 multiply_convert_fusion.2
  296.0 1.2 copy.36
  297.1 21.8 %all-to-all-done.9 = bf16[8,256,256]{2,1,0:T(8,128)(2,1)S(1)} async-done(((bf16[8,256,256]{2,1,0:T(8,128)(2,1)}), bf16[8,256,256]{2,1,0:T(8,128)(2,1)S(1)}, u32[]{:S(2)}, u32[]{:S(2)}) %all-to-all-start.9) | async-done | bytes 1048608 | tf_op jit(solution)/shard_map/all_to_all | solution.py:404
  318.9 4.3 %all-to-all-start.5 = ((bf16[8,256,256]{2,1,0:T(8,128)(2,1)}), bf16[8,256,256]{2,1,0:T(8,128)(2,1)S(1)}, u32[]{:S(2)}, u32[]{:S(2)}) async-start(bf16[8,256,256]{2,1,0:T(8,128)(2,1)} %copy.36), calls=%async_computation.5 | async-start | bytes 2097152 | tf_op jit(solution)/shard_map/all_to_all | solution.py:395
  323.3 2.8 multiply_convert_fusion.3
  326.0 1.2 copy.33
  327.2 21.8 %all-to-all-done.5 = bf16[8,256,256]{2,1,0:T(8,128)(2,1)S(1)} async-done(((bf16[8,256,256]{2,1,0:T(8,128)(2,1)}), bf16[8,256,256]{2,1,0:T(8,128)(2,1)S(1)}, u32[]{:S(2)}, u32[]{:S(2)}) %all-to-all-start.5) | async-done | bytes 1048608 | tf_op jit(solution)/shard_map/all_to_all | solution.py:395
  349.0 4.3 %all-to-all-start.3 = ((bf16[8,256,256]{2,1,0:T(8,128)(2,1)}), bf16[8,256,256]{2,1,0:T(8,128)(2,1)S(1)}, u32[]{:S(2)}, u32[]{:S(2)}) async-start(bf16[8,256,256]{2,1,0:T(8,128)(2,1)} %copy.33), calls=%async_computation.3 | async-start | bytes 2097152 | tf_op jit(solution)/shard_map/all_to_all | solution.py:377
  353.3 2.8 multiply_convert_fusion.1
  356.1 1.2 copy.39
  357.3 21.8 %all-to-all-done.3 = bf16[8,256,256]{2,1,0:T(8,128)(2,1)S(1)} async-done(((bf16[8,256,256]{2,1,0:T(8,128)(2,1)}), bf16[8,256,256]{2,1,0:T(8,128)(2,1)S(1)}, u32[]{:S(2)}, u32[]{:S(2)}) %all-to-all-start.3) | async-done | bytes 1048608 | tf_op jit(solution)/shard_map/all_to_all | solution.py:377
  379.1 1.0 copy-done.3
  380.1 4.3 %all-to-all-start.7 = ((bf16[8,256,256]{2,1,0:T(8,128)(2,1)}), bf16[8,256,256]{2,1,0:T(8,128)(2,1)S(1)}, u32[]{:S(2)}, u32[]{:S(2)}) async-start(bf16[8,256,256]{2,1,0:T(8,128)(2,1)} %copy.39), calls=%async_computation.7 | async-start | bytes 2097152 | tf_op jit(solution)/shard_map/all_to_all | solution.py:386
  384.4 1.3 stack_reshape.15
  385.7 2.7 maximum_bitcast_fusion
  388.4 21.7 %all-to-all-done.7 = bf16[8,256,256]{2,1,0:T(8,128)(2,1)S(1)} async-done(((bf16[8,256,256]{2,1,0:T(8,128)(2,1)}), bf16[8,256,256]{2,1,0:T(8,128)(2,1)S(1)}, u32[]{:S(2)}, u32[]{:S(2)}) %all-to-all-start.7) | async-done | bytes 1048608 | tf_op jit(solution)/shard_map/all_to_all | solution.py:386
  410.1 0.5 stack_reshape.14
  410.7 1.5 maximum_bitcast_fusion.1
  (30 shorter events, 0.2 us)
Async XLA Ops:
  0.6 1.6 copy-start
  3.1 12.5 %all-to-all-start = ((bf16[8,2,2048]{2,1,0:T(2,128)(2,1)}), bf16[8,2,2048]{2,1,0:T(2,128)(2,1)S(1)}, u32[]{:S(2)}, u32[]{:S(2)}) async-start(bf16[8,2,2048]{2,1,0:T(2,128)(2,1)} %reshape.104), calls=%async_computation | async-start | bytes 131072 | tf_op jit(solution)/shard_map/all_to_all | solution.py:336
  15.5 9.2 %all-to-all-start.1 = ((bf16[8,2,2048]{2,1,0:T(2,128)(2,1)}), bf16[8,2,2048]{2,1,0:T(2,128)(2,1)S(1)}, u32[]{:S(2)}, u32[]{:S(2)}) async-start(bf16[8,2,2048]{2,1,0:T(2,128)(2,1)} %reshape.105), calls=%async_computation.1 | async-start | bytes 131072 | tf_op jit(solution)/shard_map/all_to_all | solution.py:337
  62.3 4.2 %copy-start.1 = (bf16[2,4,4,16,2048]{4,3,2,1,0:T(8,128)(2,1)}, bf16[2,4,4,16,2048]{4,3,2,1,0:T(8,128)(2,1)S(1)}, u32[]{:S(2)}) copy-start(bf16[2,4,4,16,2048]{4,3,2,1,0:T(8,128)(2,1)S(1)} %get-tuple-element.4) | copy-start | bytes 6291460
  62.3 53.1 %copy-start.2 = (bf16[2,4,4,16,2048]{4,3,2,1,0:T(8,128)(2,1)}, bf16[2,4,4,16,2048]{4,3,2,1,0:T(8,128)(2,1)S(1)}, u32[]{:S(2)}) copy-start(bf16[2,4,4,16,2048]{4,3,2,1,0:T(8,128)(2,1)S(1)} %get-tuple-element.5) | copy-start | bytes 6291460
  62.3 3.4 copy-start.6
  65.7 24.6 %copy-start.7 = (f32[512,256]{1,0:T(8,128)}, f32[512,256]{1,0:T(8,128)S(1)}, u32[]{:S(2)}) copy-start(f32[512,256]{1,0:T(8,128)S(1)} %fusion.14) | copy-start | bytes 1572868
  66.5 48.1 %copy-start.8 = (bf16[1,2,2048,256]{3,2,1,0:T(8,128)(2,1)S(1)}, bf16[1,2,2048,256]{3,2,1,0:T(8,128)(2,1)}, u32[]{:S(2)}) copy-start(bf16[1,2,2048,256]{3,2,1,0:T(8,128)(2,1)} %param.11) | copy-start | bytes 6291460
  115.3 0.8 copy-start.12
  118.2 39.8 %all-to-all-start.8 = ((bf16[8,256,256]{2,1,0:T(8,128)(2,1)}), bf16[8,256,256]{2,1,0:T(8,128)(2,1)S(1)}, u32[]{:S(2)}, u32[]{:S(2)}) async-start(bf16[8,256,256]{2,1,0:T(8,128)(2,1)} %reshape.116), calls=%async_computation.8 | async-start | bytes 2097152 | tf_op jit(solution)/shard_map/all_to_all | solution.py:406
  135.2 0.7 copy-start.10
  137.7 25.4 %copy-start.9 = (bf16[1,2,2048,256]{3,2,1,0:T(8,128)(2,1)S(1)}, bf16[1,2,2048,256]{3,2,1,0:T(8,128)(2,1)}, u32[]{:S(2)}) copy-start(bf16[1,2,2048,256]{3,2,1,0:T(8,128)(2,1)} %param.11) | copy-start | bytes 6291460
  158.1 59.9 %all-to-all-start.4 = ((bf16[8,256,256]{2,1,0:T(8,128)(2,1)}), bf16[8,256,256]{2,1,0:T(8,128)(2,1)}, u32[]{:S(2)}, u32[]{:S(2)}) async-start(bf16[8,256,256]{2,1,0:T(8,128)(2,1)} %bitcast.76), calls=%async_computation.4 | async-start | bytes 2097152 | tf_op jit(solution)/shard_map/all_to_all | solution.py:397
  218.0 40.8 %all-to-all-start.2 = ((bf16[8,256,256]{2,1,0:T(8,128)(2,1)}), bf16[8,256,256]{2,1,0:T(8,128)(2,1)}, u32[]{:S(2)}, u32[]{:S(2)}) async-start(bf16[8,256,256]{2,1,0:T(8,128)(2,1)} %bitcast.77), calls=%async_computation.2 | async-start | bytes 2097152 | tf_op jit(solution)/shard_map/all_to_all | solution.py:379
  235.7 27.4 %copy-start.11 = (s32[2,8]{1,0:T(2,128)S(1)}, s32[2,8]{1,0:T(2,128)}, u32[]{:S(2)}) copy-start(s32[2,8]{1,0:T(2,128)} %param.13) | copy-start | bytes 196
  258.8 30.1 %all-to-all-start.6 = ((bf16[8,256,256]{2,1,0:T(8,128)(2,1)}), bf16[8,256,256]{2,1,0:T(8,128)(2,1)S(1)}, u32[]{:S(2)}, u32[]{:S(2)}) async-start(bf16[8,256,256]{2,1,0:T(8,128)(2,1)} %reshape.115), calls=%async_computation.6 | async-start | bytes 2097152 | tf_op jit(solution)/shard_map/all_to_all | solution.py:388
  288.8 30.1 %copy-start.5 = (bf16[8,256,256]{2,1,0:T(8,128)(2,1)}, bf16[8,256,256]{2,1,0:T(8,128)(2,1)S(1)}, u32[]{:S(2)}) copy-start(bf16[8,256,256]{2,1,0:T(8,128)(2,1)S(1)} %all-to-all-done.6) | copy-start | bytes 3145732
  288.8 30.1 %all-to-all-start.9 = ((bf16[8,256,256]{2,1,0:T(8,128)(2,1)}), bf16[8,256,256]{2,1,0:T(8,128)(2,1)S(1)}, u32[]{:S(2)}, u32[]{:S(2)}) async-start(bf16[8,256,256]{2,1,0:T(8,128)(2,1)} %copy.42), calls=%async_computation.9 | async-start | bytes 2097152 | tf_op jit(solution)/shard_map/all_to_all | solution.py:404
  318.9 30.1 %all-to-all-start.5 = ((bf16[8,256,256]{2,1,0:T(8,128)(2,1)}), bf16[8,256,256]{2,1,0:T(8,128)(2,1)S(1)}, u32[]{:S(2)}, u32[]{:S(2)}) async-start(bf16[8,256,256]{2,1,0:T(8,128)(2,1)} %copy.36), calls=%async_computation.5 | async-start | bytes 2097152 | tf_op jit(solution)/shard_map/all_to_all | solution.py:395
  349.0 30.1 %all-to-all-start.3 = ((bf16[8,256,256]{2,1,0:T(8,128)(2,1)}), bf16[8,256,256]{2,1,0:T(8,128)(2,1)S(1)}, u32[]{:S(2)}, u32[]{:S(2)}) async-start(bf16[8,256,256]{2,1,0:T(8,128)(2,1)} %copy.33), calls=%async_computation.3 | async-start | bytes 2097152 | tf_op jit(solution)/shard_map/all_to_all | solution.py:377
  379.1 1.0 copy-start.3
  380.1 30.1 %all-to-all-start.7 = ((bf16[8,256,256]{2,1,0:T(8,128)(2,1)}), bf16[8,256,256]{2,1,0:T(8,128)(2,1)S(1)}, u32[]{:S(2)}, u32[]{:S(2)}) async-start(bf16[8,256,256]{2,1,0:T(8,128)(2,1)} %copy.39), calls=%async_computation.7 | async-start | bytes 2097152 | tf_op jit(solution)/shard_map/all_to_all | solution.py:386
  388.4 22.2 %copy-start.4 = (bf16[1,256,2048]{2,1,0:T(8,128)(2,1)S(1)}, bf16[1,256,2048]{2,1,0:T(8,128)(2,1)}, u32[]{:S(2)}) copy-start(bf16[1,256,2048]{2,1,0:T(8,128)(2,1)} %stack_reshape.15) | copy-start | bytes 3145732

commit v2 on v1

v2 whole, which is shorter than its diff:
```python
import jax
import jax.numpy as jnp
from jax import lax
from jax.experimental import pallas as pl
from jax.experimental.pallas import tpu as pltpu
from jax.sharding import PartitionSpec as P

SLOTS = 16
MESH = pl.DeviceIdType.MESH
BF = jnp.bfloat16
F32 = jnp.float32
WIDTH = 2048
HALF = 1024
QUARTER = 512
HIDDEN = 256
ROWS = 512
PLANE = 256
COPIES = 420
RATE = 90000.0
DELAY = 2.5
SIDE_LAG = 3.0


class Wires:
    def __init__(self, plan, send, recv):
        self.plan, self.send, self.recv, self.made = plan, send, recv, []
        path = lax.axis_index("path")
        self.path = path
        self.zl, self.core = path // 2, lax.rem(path, 2)
        self.z_two = lax.rem(self.zl + 2, 4)
        self.z_one = self.zl + 1 - 2 * lax.rem(self.zl, 2)
        self.z_three = lax.rem(self.z_one + 2, 4)
        shard = lax.axis_index("shard")
        self.zh = shard // 16
        self.x = lax.rem(shard // 4, 4)
        self.y = lax.rem(shard, 4)

    def shard(self, zh, x, y):
        return {"shard": zh * 16 + x * 4 + y}

    def xs(self, step):
        return lax.rem(self.x + step + 4, 4)

    def ys(self, step):
        return lax.rem(self.y + step + 4, 4)

    def pos(self, axis, step):
        return self.xs(step) if axis == "x" else self.ys(step)

    def beside(self, axis, step):
        if axis == "x":
            to = self.shard(self.zh, self.xs(step), self.y)
        else:
            to = self.shard(self.zh, self.x, self.ys(step))
        ways = {1: "+", -1: "-", 2: "+-"}[step]
        return to, [(axis + way, 2.0) for way in ways]

    def across(self):
        return self.shard(1 - self.zh, self.x, self.y), [("z", 4.0), ("far", 0.0)]

    def level_with(self, z, load):
        return {"path": z * 2 + self.core}, [("z", load)]

    def sibling(self):
        return {"path": self.zl * 2 + 1 - self.core}, [("core", 0.4)]

    def peers(self):
        for dz in range(4):
            for dc in range(2):
                if dz or dc:
                    core = lax.rem(self.core + dc, 2)
                    yield lax.rem(self.zl + dz, 4) * 2 + core

    def push(self, src, dst, where):
        to, links = where
        k = len(self.made)
        copy = pltpu.make_async_remote_copy(
            src_ref=src,
            dst_ref=dst,
            send_sem=self.send.at[k],
            recv_sem=self.recv.at[k],
            device_id=to,
            device_id_type=MESH,
        )
        copy.start()
        size = 2
        for extent in src.shape:
            size *= extent
        self.made.append(copy)
        self.plan.sent(copy, size, links)
        return copy

    def drain(self):
        for copy in self.made:
            copy.wait_send()

    def greet(self, meanwhile):
        barrier = pltpu.get_barrier_semaphore()
        peers = [self.beside(axis, step)[0] for axis in "xy" for step in (1, -1, 2)]
        peers += [self.across()[0]] + [{"path": to} for to in self.peers()]
        for to in peers:
            pl.semaphore_signal(barrier, inc=1, device_id=to, device_id_type=MESH)
        meanwhile()
        pl.semaphore_wait(barrier, len(peers))


class Plan:
    def __init__(self):
        self.clock, self.free, self.due, self.marks = 0.0, {}, {}, {}

    def sent(self, copy, size, links):
        end = self.clock
        for name, load in links:
            if name == "far":
                end += 1.5
                continue
            start = max(self.clock, self.free.get(name, 0.0))
            self.free[name] = start + size * load / RATE
            end = max(end, self.free[name])
        self.due[id(copy)] = end + DELAY
        self.clock += 0.08

    def work(self, time):
        self.clock += time

    def mark(self, name):
        self.marks.setdefault(name, []).append(self.clock)

    def need(self, *names):
        yield "marks", names

    def ready(self, state):
        kind, items = state
        if kind == "copies":
            return max(self.due[id(copy)] for copy in items)
        times = [0.0]
        for name, count in items:
            have = self.marks.get(name, [])
            if len(have) < count:
                return None
            times.append(have[count - 1])
        return max(times)

    def run(self, tasks):
        tasks = [[lag, task, None] for lag, task in tasks]
        for entry in tasks:
            entry[2] = next(entry[1])
        while tasks:
            best = None
            for entry in tasks:
                time = self.ready(entry[2])
                if time is None:
                    continue
                time = max(time + entry[0], self.clock)
                if best is None or time < best[0] - 1e-6:
                    best = (time, entry)
            time, entry = best
            self.clock = max(self.clock, self.ready(entry[2]))
            try:
                entry[2] = next(entry[1])
            except StopIteration:
                tasks.remove(entry)


def ring_gather(w, axis, view, low, size):
    here, left, right = w.pos(axis, 0), w.pos(axis, -1), w.pos(axis, 1)
    own = view(here, low, size)
    go_right = w.push(own, own, w.beside(axis, 1))
    go_left = w.push(own, own, w.beside(axis, -1))
    yield "copies", [go_right]
    go_right.wait_recv()
    part = view(left, low, size // 2)
    on_right = w.push(part, part, w.beside(axis, 1))
    yield "copies", [go_left]
    go_left.wait_recv()
    part = view(right, low + size // 2, size // 2)
    on_left = w.push(part, part, w.beside(axis, -1))
    yield "copies", [on_right, on_left]
    on_right.wait_recv()
    on_left.wait_recv()


def ring_share(w, axis, view, low, size):
    own = view(w.pos(axis, 0), low, size)
    sent = [w.push(own, own, w.beside(axis, step)) for step in (1, -1, 2)]
    yield "copies", sent
    for copy in sent:
        copy.wait_recv()


def gather(w, plan, full, name, after):
    over, waited = [], []

    def half(mine, first, second, low):
        plane = w.zh if mine else 1 - w.zh
        yield from plan.need(*after)
        if not over:
            own = full.at[w.zh, w.x, w.y]
            over.append(w.push(own, own, w.across()))
        if not mine:
            yield "copies", over
            if not waited:
                over[0].wait_recv()
                waited.append(True)

        def line(i, start, size):
            cols = pl.ds(start, size)
            if first == "x":
                return full.at[plane, i, w.y, :, cols]
            return full.at[plane, w.x, i, :, cols]

        def sheet(i, start, size):
            cols = pl.ds(start, size)
            if second == "x":
                return full.at[plane, i, :, :, cols]
            return full.at[plane, :, i, :, cols]

        yield from ring_share(w, first, line, low, HALF)
        yield from ring_gather(w, second, sheet, low, HALF)
        plan.mark((name, mine))

    return [
        half(True, "x", "y", 0),
        half(True, "y", "x", HALF),
        half(False, "x", "y", 0),
        half(False, "y", "x", HALF),
    ]


def path_gather(w, plan, view, name, after):
    def block(z):
        return view(z * 2 + w.core)

    yield from plan.need(*after)
    own = block(w.zl)
    two = w.push(own, own, w.level_with(w.z_two, 4.0))
    one = w.push(own, own, w.level_with(w.z_one, 2.0))
    aside = [w.push(own, own, w.sibling())]
    yield "copies", [two]
    two.wait_recv()
    got = block(w.z_two)
    three = w.push(got, got, w.level_with(w.z_one, 2.0))
    aside.append(w.push(got, got, w.sibling()))
    yield "copies", [one]
    one.wait_recv()
    got = block(w.z_one)
    aside.append(w.push(got, got, w.sibling()))
    yield "copies", [three]
    three.wait_recv()
    got = block(w.z_three)
    aside.append(w.push(got, got, w.sibling()))
    yield "copies", aside
    for copy in aside:
        copy.wait_recv()
    plan.mark(name)


def ring_reduce(w, axis, view, low, bufs, out):
    from_left, from_right, in_r_lo, in_r_hi, in_l_lo, in_l_hi, tmp_r, tmp_l = bufs
    q = QUARTER
    here, left, right, far = (w.pos(axis, s) for s in (0, -1, 1, 2))
    to_right, to_left = w.beside(axis, 1), w.beside(axis, -1)
    a = w.push(view(far, low, q), from_left, to_right)
    b = w.push(view(far, low + q, q), from_right, to_left)
    c = w.push(view(right, low + q, q), in_r_hi, to_right)
    d = w.push(view(left, low, q), in_l_lo, to_left)
    yield "copies", [a]
    a.wait_recv()
    tmp_r[...] = (view(right, low, q)[...].astype(F32) + from_left[...].astype(F32)).astype(BF)
    w.plan.work(0.2)
    e = w.push(tmp_r, in_r_lo, to_right)
    yield "copies", [b]
    b.wait_recv()
    tmp_l[...] = (view(left, low + q, q)[...].astype(F32) + from_right[...].astype(F32)).astype(BF)
    w.plan.work(0.2)
    f = w.push(tmp_l, in_l_hi, to_left)
    yield "copies", [c, d, e, f]
    for copy in (c, d, e, f):
        copy.wait_recv()
    out(0, view(here, low, q)[...].astype(F32) + in_r_lo[...].astype(F32) + in_l_lo[...].astype(F32))
    out(
        1,
        view(here, low + q, q)[...].astype(F32)
        + in_r_hi[...].astype(F32)
        + in_l_hi[...].astype(F32),
    )
    w.plan.work(0.4)


def ring_total(w, axis, view, bufs, out):
    sent = [
        w.push(view(w.pos(axis, step)), buf, w.beside(axis, step))
        for step, buf in zip((1, -1, 2), bufs)
    ]
    yield "copies", sent
    for copy in sent:
        copy.wait_recv()
    value = view(w.pos(axis, 0))[...].astype(F32)
    for buf in bufs:
        value = value + buf[...].astype(F32)
    out(value)
    w.plan.work(0.2)


def reduce(w, plan, part, scratch, name, after):
    big, small, mid, far, near, total = scratch
    over = {}

    def half(k, mine, first, second, low):
        plane = w.zh if mine else 1 - w.zh
        yield from plan.need(((after, mine), 1))

        def sheet(i, start, size):
            cols = pl.ds(start, size)
            if first == "x":
                return part.at[plane, i, :, :, cols]
            return part.at[plane, :, i, :, cols]

        def keep(which, value):
            mid[k, :, :, pl.ds(which * QUARTER, QUARTER)] = value.astype(BF)

        def line(i):
            return mid.at[k, i]

        def last(value):
            cols = pl.ds(low, HALF)
            if mine:
                total[:, cols] = value
            else:
                far[:, cols] = value.astype(BF)

        yield from ring_reduce(w, first, sheet, low, [big.at[k, n] for n in range(8)], keep)
        yield from ring_total(w, second, line, [small.at[k, n] for n in range(3)], last)
        if not mine:
            cols = pl.ds(low, HALF)
            over[low] = w.push(far.at[:, cols], near.at[:, cols], w.across())
        plan.mark(name + "_part")

    def finish():
        yield from plan.need((name + "_part", 4))
        yield "copies", [over[0], over[HALF]]
        for low in (0, HALF):
            over[low].wait_recv()
            cols = pl.ds(low, HALF)
            total[:, cols] = total[:, cols] + near[:, cols].astype(F32)
        plan.mark(name)

    return [
        half(0, False, "x", "y", 0),
        half(1, False, "y", "x", HALF),
        half(2, True, "x", "y", 0),
        half(3, True, "y", "x", HALF),
        finish(),
    ]


def reduce_scratch():
    return [
        pltpu.VMEM((4, 8, 4, SLOTS, QUARTER), BF),
        pltpu.VMEM((4, 3, SLOTS, HALF), BF),
        pltpu.VMEM((4, 4, SLOTS, HALF), BF),
        pltpu.VMEM((SLOTS, WIDTH), BF),
        pltpu.VMEM((SLOTS, WIDTH), BF),
        pltpu.VMEM((SLOTS, WIDTH), F32),
    ]


def norm_rows(v, gain):
    return v * lax.rsqrt(jnp.mean(v * v, axis=-1, keepdims=True) + 1e-05) * gain.astype(F32)


def norm_pull(v, gain, grad):
    turn = lax.rsqrt(jnp.mean(v * v, axis=-1, keepdims=True) + 1e-05)
    scaled = grad * gain.astype(F32)
    along = jnp.mean(scaled * v, axis=-1, keepdims=True)
    return turn * scaled - v * (turn * turn * turn * along)


def gelu_both(a):
    c = 0.7978845608028654
    square = a * a
    t = jnp.tanh(c * (a + 0.044715 * a * square))
    value = 0.5 * a * (1.0 + t)
    slope = 0.5 * (1.0 + t) + 0.5 * a * (1.0 - t * t) * (c * (1.0 + 3.0 * 0.044715 * square))
    return value, slope


def dot(a, b):
    return jnp.dot(a, b, preferred_element_type=F32)


def dot_t(a, b):
    return lax.dot_general(a, b, (((1,), (1,)), ((), ())), preferred_element_type=F32)


def step_kernel(
    partners,
    tokens,
    routes,
    cotangent,
    gains,
    w_in,
    w_out,
    d_in,
    d_out,
    packed,
    got,
    x_own,
    dy_own,
    wi,
    wo,
    n1,
    n2,
    dh,
    side,
    n2q,
    dhq,
    r_n1,
    r_dy,
    r_n2,
    r_dh,
    f_u1,
    f_a1,
    f_u2,
    f_a2,
    slope1,
    slope2,
    pull2,
    own_part,
    part1,
    part2,
    *rest,
):
    red1, red2 = rest[0:6], rest[6:12]
    load, send, recv = rest[12:]
    plan = Plan()
    w = Wires(plan, send, recv)
    me = w.path
    mate_low, mate_high = partners[0, me], partners[1, me]
    scale = 1.0 / jnp.sqrt(jnp.float32(ROWS))
    loads = [
        pltpu.make_async_copy(w_in.at[0], wi, load.at[0]),
        pltpu.make_async_copy(w_out.at[0], wo, load.at[1]),
    ]
    for copy in loads:
        copy.start()

    def pack():
        count = tokens.shape[0]
        route = routes[...]
        named = (route == lax.broadcasted_iota(jnp.int32, (count, 128), 1)).astype(BF)
        same = dot_t(named, named)
        before = lax.broadcasted_iota(jnp.int32, same.shape, 1) < lax.broadcasted_iota(
            jnp.int32, same.shape, 0
        )
        rank = jnp.sum(jnp.where(before, same, 0.0), axis=1, keepdims=True)
        place = route.astype(F32) * 2.0 + rank
        slot = lax.broadcasted_iota(jnp.int32, (count, SLOTS), 1).astype(F32)
        select = (place == slot).astype(BF)
        for k, rows in enumerate((tokens, cotangent)):
            sorted_rows = lax.dot_general(
                select, rows[...], (((0,), (0,)), ((), ())), preferred_element_type=F32
            )
            for p in range(8):
                packed[p, k] = sorted_rows[2 * p : 2 * p + 2].astype(BF)

    w.greet(pack)
    hops = [w.push(packed.at[to], got.at[me], ({"path": to}, [("z", 0.0)])) for to in w.peers()]
    got[me] = packed[me]
    for copy in hops:
        copy.wait_recv()
    for p in range(8):
        x_own[2 * p : 2 * p + 2, :] = got[p, 0].astype(F32)
        dy_own[2 * p : 2 * p + 2, :] = got[p, 1].astype(F32)
    rows_n1 = norm_rows(x_own[...], gains[0, 0:1, :]).astype(BF)
    n1[w.zh, w.x, w.y] = rows_n1
    r_n1[me] = rows_n1
    rows_dy = dy_own[...].astype(BF)
    r_dy[me] = rows_dy
    side[w.zh, w.x, w.y, 0:SLOTS] = rows_dy

    def plane_of(mine):
        return w.zh if mine else 1 - w.zh

    def load_weights():
        yield from plan.need()
        for copy in loads:
            copy.wait()
        plan.mark("weights")

    def side_rows():
        yield from plan.need(("r_n1", 1), ("r_dy", 1))
        side[w.zh, w.x, w.y, SLOTS : 2 * SLOTS] = r_n1[mate_low]
        side[w.zh, w.x, w.y, 2 * SLOTS : 3 * SLOTS] = r_dy[mate_high]
        plan.mark("side_rows")

    def first(mine):
        p = plane_of(mine)
        yield from plan.need((("n1", mine), 2), ("weights", 1))
        a = dot(n1[p].reshape(PLANE, WIDTH), wi[0])
        value, slope = gelu_both(a)
        u = value.astype(BF)
        slope1[p] = slope
        f_u1[me, p] = u
        for c in range(0, WIDTH, QUARTER):
            y = dot(u, wo[0, :, c : c + QUARTER]).astype(BF)
            part1[p, :, :, :, c : c + QUARTER] = y.reshape(4, 4, SLOTS, QUARTER)
        plan.work(2.0)
        plan.mark(("part1", mine))
        plan.mark("u1")

    def middle():
        yield from plan.need(("red1", 1))
        h = (x_own[...] + red1[5][...]).astype(BF).astype(F32)
        rows = norm_rows(h, gains[0, 1:2, :]).astype(BF)
        n2[w.zh, w.x, w.y] = rows
        r_n2[me] = rows
        plan.work(0.6)
        plan.mark("n2_own")

    def pull(mine):
        p = plane_of(mine)
        yield from plan.need((("side", mine), 2), ("weights", 1))
        pull2[p] = dot_t(side[p, :, :, 0:SLOTS, :].reshape(PLANE, WIDTH), wo[1])
        plan.work(0.8)
        plan.mark(("pull2", mine))

    def second(mine):
        p = plane_of(mine)
        yield from plan.need((("n2", mine), 2), (("pull2", mine), 1))
        a = dot(n2[p].reshape(PLANE, WIDTH), wi[1])
        value, slope = gelu_both(a)
        f_u2[me, p] = value.astype(BF)
        da = (pull2[p] * slope).astype(BF)
        f_a2[me, p] = da
        for c in range(0, WIDTH, QUARTER):
            y = dot_t(da, wi[1, c : c + QUARTER, :]).astype(BF)
            part2[p, :, :, :, c : c + QUARTER] = y.reshape(4, 4, SLOTS, QUARTER)
        plan.work(2.0)
        plan.mark(("part2", mine))
        plan.mark("u2")

    def side_n2():
        yield from plan.need(("r_n2", 1))
        n2q[w.zh, w.x, w.y] = r_n2[mate_high]
        plan.mark("n2q_own")

    def back():
        yield from plan.need(("red2", 1))
        h = (x_own[...] + red1[5][...]).astype(BF).astype(F32)
        grad = norm_pull(h, gains[0, 1:2, :], red2[5][...])
        rows = (dy_own[...] + grad).astype(BF)
        dh[w.zh, w.x, w.y] = rows
        r_dh[me] = rows
        plan.work(0.8)
        plan.mark("dh_own")

    def side_dh():
        yield from plan.need(("r_dh", 1))
        dhq[w.zh, w.x, w.y] = r_dh[mate_low]
        plan.mark("dhq_own")

    def third(mine):
        p = plane_of(mine)
        yield from plan.need((("dh", mine), 2))
        du = dot_t(dh[p].reshape(PLANE, WIDTH), wo[0])
        f_a1[me, p] = (du * slope1[p]).astype(BF)
        plan.work(0.8)
        plan.mark(("a1", mine))

    def delta(out, level, k, own, mate, own_rows, mate_rows, own_needs, mate_needs, turned):
        def product(factor, rows, cols):
            return (-dot(factor, rows(cols)) * scale).astype(BF)

        def first_part():
            yield from plan.need(*own_needs)
            factor = own[me].reshape(ROWS, HIDDEN).T
            for c in range(0, WIDTH, QUARTER):
                cols = slice(c, c + QUARTER)
                own_part[k, :, cols] = product(factor, own_rows, cols)
                plan.work(0.5)
                yield from plan.need()
            plan.mark(("delta", k))

        def second_part():
            yield from plan.need((("delta", k), 1), *mate_needs)
            factor = own[mate].reshape(ROWS, HIDDEN).T
            for c in range(0, WIDTH, QUARTER):
                cols = slice(c, c + QUARTER)
                there = product(factor, mate_rows, cols).astype(F32)
                mean = ((own_part[k, :, cols].astype(F32) + there) * 0.5).astype(BF)
                if turned:
                    out[level, cols, :] = mean.T
                else:
                    out[level, :, cols] = mean
                plan.work(0.6)
                yield from plan.need()

        return [first_part(), second_part()]

    def of(ref):
        return lambda cols: ref[:, :, :, :, cols].reshape(ROWS, QUARTER)

    def of_side(k):
        return lambda cols: side[:, :, :, k * SLOTS : (k + 1) * SLOTS, cols].reshape(ROWS, QUARTER)

    def both(name):
        return [((name, True), 2), ((name, False), 2)]

    def spread(f, name, after):
        return [
            path_gather(
                w,
                plan,
                lambda q, p=plane_of(mine): f.at[q, p],
                name,
                [((after, mine), 1)],
            )
            for mine in (True, False)
        ]

    main = [load_weights()]
    main += gather(w, plan, n1, "n1", [])
    main += [first(True), first(False)]
    main += reduce(w, plan, part1, red1, "red1", "part1")
    main += [middle()]
    main += gather(w, plan, n2, "n2", [("n2_own", 1)])
    main += [second(True), second(False)]
    main += reduce(w, plan, part2, red2, "red2", "part2")
    main += [back()]
    main += gather(w, plan, dh, "dh", [("dh_own", 1)])
    main += [third(True), third(False)]
    tail = [path_gather(w, plan, lambda q: r_dh.at[q], "r_dh", [("dh_own", 1)]), side_dh()]
    tail += gather(w, plan, dhq, "dhq", [("dhq_own", 1)])
    tail += spread(f_a1, "f_a1", "a1")
    low = [path_gather(w, plan, lambda q: r_dy.at[q], "r_dy", [])]
    low += [path_gather(w, plan, lambda q: r_n1.at[q], "r_n1", [])]
    low += [side_rows()]
    low += gather(w, plan, side, "side", [("side_rows", 1)])
    low += [pull(True), pull(False)]
    low += spread(f_u1, "f_u1", "part1")
    low += [path_gather(w, plan, lambda q: r_n2.at[q], "r_n2", [("n2_own", 1)]), side_n2()]
    low += spread(f_u2, "f_u2", "part2")
    low += spread(f_a2, "f_a2", "part2")
    low += gather(w, plan, n2q, "n2q", [("n2q_own", 1)])

    high_out = delta(
        d_out, 1, 0, f_u2, mate_high, of_side(0), of_side(2),
        both("side") + [(("part2", True), 1), (("part2", False), 1)], [("f_u2", 2)], False,
    )
    high_in = delta(
        d_in, 1, 1, f_a2, mate_high, of(n2), of(n2q),
        both("n2") + [(("part2", True), 1), (("part2", False), 1)], [("f_a2", 2)] + both("n2q"), True,
    )
    low_out = delta(
        d_out, 0, 2, f_u1, mate_low, of(dh), of(dhq),
        both("dh"), [("f_u1", 2)] + both("dhq"), False,
    )
    low_in = delta(
        d_in, 0, 3, f_a1, mate_low, of(n1), of_side(1),
        [(("a1", True), 1), (("a1", False), 1)], [("f_a1", 2)] + both("side"), True,
    )
    low += high_out + high_in
    tail += low_out + low_in
    plan.run([(0.0, t) for t in main] + [(0.5, t) for t in tail] + [(SIDE_LAG, t) for t in low])
    w.drain()


def step_call(tokens, routes, cotangent, gains, w_in, w_out, partners):
    anywhere = pl.BlockSpec(memory_space=pl.ANY)
    vmem = pl.BlockSpec(memory_space=pltpu.VMEM)

    def full(rows):
        return pltpu.VMEM((2, 4, 4, rows, WIDTH), BF)

    def by_path():
        return pltpu.VMEM((8, SLOTS, WIDTH), BF)

    def factor():
        return pltpu.VMEM((8, 2, PLANE, HIDDEN), BF)

    return pl.pallas_call(
        step_kernel,
        out_shape=[
            jax.ShapeDtypeStruct((2, WIDTH, HIDDEN), BF),
            jax.ShapeDtypeStruct((2, HIDDEN, WIDTH), BF),
        ],
        in_specs=[pl.BlockSpec(memory_space=pltpu.SMEM)] + [vmem] * 4 + [anywhere] * 2,
        out_specs=[vmem, vmem],
        scratch_shapes=[
            pltpu.VMEM((8, 2, 2, WIDTH), BF),
            pltpu.VMEM((8, 2, 2, WIDTH), BF),
            pltpu.VMEM((SLOTS, WIDTH), F32),
            pltpu.VMEM((SLOTS, WIDTH), F32),
            pltpu.VMEM((2, WIDTH, HIDDEN), BF),
            pltpu.VMEM((2, HIDDEN, WIDTH), BF),
            full(SLOTS),
            full(SLOTS),
            full(SLOTS),
            full(3 * SLOTS),
            full(SLOTS),
            full(SLOTS),
            by_path(),
            by_path(),
            by_path(),
            by_path(),
            factor(),
            factor(),
            factor(),
            factor(),
            pltpu.VMEM((2, PLANE, HIDDEN), F32),
            pltpu.VMEM((2, PLANE, HIDDEN), F32),
            pltpu.VMEM((2, PLANE, HIDDEN), F32),
            pltpu.VMEM((4, HIDDEN, WIDTH), BF),
            full(SLOTS),
            full(SLOTS),
        ]
        + reduce_scratch()
        + reduce_scratch()
        + [
            pltpu.SemaphoreType.DMA((2,)),
            pltpu.SemaphoreType.DMA((COPIES,)),
            pltpu.SemaphoreType.DMA((COPIES,)),
        ],
        compiler_params=pltpu.CompilerParams(
            collective_id=0, has_side_effects=True, vmem_limit_bytes=62 << 20
        ),
    )(partners, tokens, routes, cotangent, gains, w_in, w_out)


def body(tokens, routes, cotangent, gains, w_in, w_out, partners):
    d_in, d_out = step_call(tokens, routes, cotangent, gains, w_in, w_out, partners)
    return d_in[None], d_out[None]


def solution(mesh):
    in_specs = (
        P(("path", "shard"), None),
        P(("path", "shard"), None),
        P(("path", "shard"), None),
        P("path", None, None),
        P("path", None, None, "shard"),
        P("path", None, "shard", None),
        P(),
    )
    out_specs = (P("path", None, None, "shard"), P("path", None, "shard", None))
    return jax.shard_map(body, mesh=mesh, in_specs=in_specs, out_specs=out_specs, check_vma=False)
```

time: 413 us -> 187 us (0.45)
  waiting for transfers between devices: 159 us -> 0 us
  starting transfers between devices: 67.2 us -> 0 us
  Pallas kernels: 133 us -> 180 us
  matrix products: 30.5 us -> 0 us
  local copies, waits for them, and re-layouts: 14.7 us -> 5.85 us
  other arithmetic: 7.33 us -> 0 us
    all_to_all x10 -> x0, waiting for transfers between devices: 159 us -> none  [the longest x1 23.3 us: body(): lax.all_to_all(e_out1, 'path', split_axis=0, concat_axis=0, tiled=True)]
    all_to_all x10 -> x0, starting transfers between devices: 67.2 us -> none  [the longest x1 15 us: body(): lax.all_to_all(e_in1, 'path', split_axis=0, concat_axis=0, tiled=True)]
    pallas_call x5 -> x1, Pallas kernels: 133 us -> 180 us  [step_call(): pl.pallas_call(step_kernel, out_shape=[jax.ShapeDtypeStruct((2, WIDTH, HI...]
    dot_general x15 -> x0, matrix products: 30.5 us -> none  [the longest x4 9.57 us: pair_mean(): jnp.einsum('pq,qrc->prc', pick, values, precision=lax.Precision.HIGHEST)]
    reshape x5 -> x0, local copies, waits for them, and re-layouts: 5.07 us -> none  [the longest x1 2.33 us: body(): (-g_out1 * scale).astype(jnp.bfloat16)]
    convert_element_type x5 -> x0, local copies, waits for them, and re-layouts: 4.72 us -> none  [the longest x4 4.7 us: pair_mean(): return ((values + other) * 0.5).astype(jnp.bfloat16)]
    broadcast_in_dim x2 -> x0, other arithmetic: 4.24 us -> none  [the longest x1 2.73 us: body(): jnp.stack([avg_in1.reshape(width, hidden), avg_in2.reshape(width, hidden)])]
  transfers between devices with their start and end apart: 10 -> 0, of which waited for: 9 -> 0; matrix products, arithmetic and copies ran while one was open for 9% -> 0% of each run, Pallas kernels for 11% -> 0%
where the time goes in v2:
time: 187 us; the launch traced here: 186 us
  Pallas kernels  180 us (96%)
  local copies, waits for them, and re-layouts  5.85 us (3%)
    pallas_call x1, Pallas kernels, step_call(): pl.pallas_call(step_kernel, out_shape=[jax.ShapeDtypeStruct((2, WIDTH, HI...  180 us
    unnamed x5, local copies, waits for them, and re-layouts  5.85 us

profile of v2, /device:TPU:1, one launch (start us, length us, event | category | flops | bytes accessed | tf_op | source)
XLA Modules:
  0.0 186.1 jit_solution(16603761836632970336)
XLA Ops:
  0.6 1.3 copy.9.routes
  2.0 179.6 %shard_map.86 = (bf16[2,2048,256]{2,1,0:T(8,128)(2,1)}, bf16[2,256,2048]{2,1,0:T(8,128)(2,1)}) custom-call(s32[2,8]{1,0:T(2,128)} %partners.1, bf16[12,2048]{1,0:T(8,128)(2,1)} %tokens.1, s32[12,1]{1,0:T(8,128)} %copy.9.routes, bf16[12,2048]{1,0:T(8,128)(2,1)} %cotangent.1, bf16[1,2,2048]{2,1,0:T(2,128)(2,1)} %gains.1, bf16[1,2,2048,256]{3,2,1,0:T(8,128)(2,1)} %w_in.1, ...), custom_call_target="tpu_custom_call" | custom-call | tf_op jit(solution)/shard_map/pallas_call | solution.py:682
  181.5 0.0 copy-start
  181.6 3.2 %copy.12 = bf16[1,2,2048,256]{3,2,1,0:T(8,128)(2,1)} copy(bf16[1,2,2048,256]{3,2,1,0:T(8,128)(2,1)} %bitcast.3) | data formatting | bytes 4194304
  184.7 0.0 copy-done
  184.7 1.3 copy.13
Async XLA Ops:
  181.5 3.2 %copy-start = (bf16[2,256,2048]{2,1,0:T(8,128)(2,1)S(1)}, bf16[2,256,2048]{2,1,0:T(8,128)(2,1)}, u32[]{:S(2)}) copy-start(bf16[2,256,2048]{2,1,0:T(8,128)(2,1)} %get-tuple-element.5) | copy-start | bytes 6291460

commit v3 on v2

--- a/solution.py
+++ b/solution.py
@@ -15,10 +15,12 @@
 HIDDEN = 256
 ROWS = 512
 PLANE = 256
-COPIES = 420
+COPIES = 480
 RATE = 90000.0
 DELAY = 2.5
-SIDE_LAG = 3.0
+DIRECT_REDUCE = False
+STRAIGHT = {'n2': (True, False), 'n2q': (True, False), 'dh': (False, False), 'n1': (True, False), 'dy': (False, False), 'side': (False, False), 'dhq': (True, False)}
+LAGS = {'dy': (29.6, 4.3), 'r_dy': (10.5, 9.6), 'r_n1': (0.1, 5.8), 'side': (23.6, 9.6), 'f_u1': (6.4, 4.3), 'r_n2': (5.9, 3.2), 'f_u2': (18.0, 3.4), 'f_a2': (2.0, 8.3), 'n2q': (3.0, 3.6), 'high': (2.8, 1.6), 'own': (9.0, 0.5), 'r_dh': (2.2, 0.1), 'dhq': (0.0, 6.8), 'f_a1': (1.2, 7.7), 'pull': (2.1, 7.0), 'second': (1.2, 3.2), 'first': (1.7, 0.0), 'end': (4.5, 5.0), 'n1': (0.0, 6.1), 'dh': (0.0, 1.1), 'red1': (2.0, 2.8), 'red2': (0.0, 0.0), 'n2': (0.0, 4.2), 'third': (4.0, 0.1)}
 
 
 class Wires:
@@ -29,7 +31,6 @@
         self.zl, self.core = path // 2, lax.rem(path, 2)
         self.z_two = lax.rem(self.zl + 2, 4)
         self.z_one = self.zl + 1 - 2 * lax.rem(self.zl, 2)
-        self.z_three = lax.rem(self.z_one + 2, 4)
         shard = lax.axis_index("shard")
         self.zh = shard // 16
         self.x = lax.rem(shard // 4, 4)
@@ -56,10 +57,10 @@
         return to, [(axis + way, 2.0) for way in ways]
 
     def across(self):
-        return self.shard(1 - self.zh, self.x, self.y), [("z", 4.0), ("far", 0.0)]
-
-    def level_with(self, z, load):
-        return {"path": z * 2 + self.core}, [("z", load)]
+        return self.shard(1 - self.zh, self.x, self.y), [("zm", 4.0), ("ze", 4.0), ("far", 0.0)]
+
+    def level_with(self, z, links):
+        return {"path": z * 2 + self.core}, links
 
     def sibling(self):
         return {"path": self.zl * 2 + 1 - self.core}, [("core", 0.4)]
@@ -97,7 +98,9 @@
     def greet(self, meanwhile):
         barrier = pltpu.get_barrier_semaphore()
         peers = [self.beside(axis, step)[0] for axis in "xy" for step in (1, -1, 2)]
-        peers += [self.across()[0]] + [{"path": to} for to in self.peers()]
+        peers += [self.across()[0]]
+        for to in self.peers():
+            peers += [{"path": to}, {"path": to, **self.across()[0]}]
         for to in peers:
             pl.semaphore_signal(barrier, inc=1, device_id=to, device_id_type=MESH)
         meanwhile()
@@ -107,6 +110,7 @@
 class Plan:
     def __init__(self):
         self.clock, self.free, self.due, self.marks = 0.0, {}, {}, {}
+        self.used, self.stall = {}, 0.0
 
     def sent(self, copy, size, links):
         end = self.clock
@@ -116,6 +120,7 @@
                 continue
             start = max(self.clock, self.free.get(name, 0.0))
             self.free[name] = start + size * load / RATE
+            self.used[name] = self.used.get(name, 0.0) + size * load / RATE
             end = max(end, self.free[name])
         self.due[id(copy)] = end + DELAY
         self.clock += 0.08
@@ -142,7 +147,7 @@
         return max(times)
 
     def run(self, tasks):
-        tasks = [[lag, task, None] for lag, task in tasks]
+        tasks = [[{"marks": early, "copies": lag}, task, None] for early, lag, task in tasks]
         for entry in tasks:
             entry[2] = next(entry[1])
         while tasks:
@@ -151,7 +156,7 @@
                 time = self.ready(entry[2])
                 if time is None:
                     continue
-                time = max(time + entry[0], self.clock)
+                time = max(time + entry[0][entry[2][0]], self.clock)
                 if best is None or time < best[0] - 1e-6:
                     best = (time, entry)
             time, entry = best
@@ -164,20 +169,25 @@
 
 def ring_gather(w, axis, view, low, size):
     here, left, right = w.pos(axis, 0), w.pos(axis, -1), w.pos(axis, 1)
-    own = view(here, low, size)
-    go_right = w.push(own, own, w.beside(axis, 1))
-    go_left = w.push(own, own, w.beside(axis, -1))
-    yield "copies", [go_right]
-    go_right.wait_recv()
-    part = view(left, low, size // 2)
-    on_right = w.push(part, part, w.beside(axis, 1))
-    yield "copies", [go_left]
-    go_left.wait_recv()
-    part = view(right, low + size // 2, size // 2)
-    on_left = w.push(part, part, w.beside(axis, -1))
-    yield "copies", [on_right, on_left]
-    on_right.wait_recv()
-    on_left.wait_recv()
+    to_right, to_left = w.beside(axis, 1), w.beside(axis, -1)
+    half = size // 2
+    first, last = view(here, low, half), view(here, low + half, half)
+    right_first = w.push(first, first, to_right)
+    left_first = w.push(last, last, to_left)
+    right_rest = w.push(last, last, to_right)
+    left_rest = w.push(first, first, to_left)
+    yield "copies", [right_first]
+    right_first.wait_recv()
+    part = view(left, low, half)
+    right_on = w.push(part, part, to_right)
+    yield "copies", [left_first]
+    left_first.wait_recv()
+    part = view(right, low + half, half)
+    left_on = w.push(part, part, to_left)
+    ends = [right_rest, left_rest, right_on, left_on]
+    yield "copies", ends
+    for copy in ends:
+        copy.wait_recv()
 
 
 def ring_share(w, axis, view, low, size):
@@ -189,19 +199,11 @@
 
 
 def gather(w, plan, full, name, after):
-    over, waited = [], []
+    straight = STRAIGHT.get(name, (True, False))
 
     def half(mine, first, second, low):
         plane = w.zh if mine else 1 - w.zh
         yield from plan.need(*after)
-        if not over:
-            own = full.at[w.zh, w.x, w.y]
-            over.append(w.push(own, own, w.across()))
-        if not mine:
-            yield "copies", over
-            if not waited:
-                over[0].wait_recv()
-                waited.append(True)
 
         def line(i, start, size):
             cols = pl.ds(start, size)
@@ -215,8 +217,8 @@
                 return full.at[plane, i, :, :, cols]
             return full.at[plane, :, i, :, cols]
 
-        yield from ring_share(w, first, line, low, HALF)
-        yield from ring_gather(w, second, sheet, low, HALF)
+        yield from (ring_share if straight[0] else ring_gather)(w, first, line, low, HALF)
+        yield from (ring_share if straight[1] else ring_gather)(w, second, sheet, low, HALF)
         plan.mark((name, mine))
 
     return [
@@ -227,31 +229,35 @@
     ]
 
 
-def path_gather(w, plan, view, name, after):
-    def block(z):
-        return view(z * 2 + w.core)
-
+class Mates:
+    def __init__(self, w, partners, level):
+        def kept(path, other):
+            mate = partners[level, path]
+            z, core = mate // 2, lax.rem(mate, 2)
+            far = 2 + core
+            return jnp.where(z == w.zl, core, jnp.where(z == w.z_two, far, other))
+
+        self.here = kept(w.path, 4)
+        self.there = kept(w.z_one * 2 + w.core, 0)
+
+
+def path_fetch(w, plan, view, load, keep, stage, mates, name, after):
     yield from plan.need(*after)
-    own = block(w.zl)
-    two = w.push(own, own, w.level_with(w.z_two, 4.0))
-    one = w.push(own, own, w.level_with(w.z_one, 2.0))
-    aside = [w.push(own, own, w.sibling())]
+    own, far = view(w.core), view(2 + w.core)
+    two = w.push(own, far, w.level_with(w.z_two, [("zm", 4.0), ("ze", 2.0)]))
+    aside = w.push(own, own, w.sibling())
     yield "copies", [two]
     two.wait_recv()
-    got = block(w.z_two)
-    three = w.push(got, got, w.level_with(w.z_one, 2.0))
-    aside.append(w.push(got, got, w.sibling()))
-    yield "copies", [one]
-    one.wait_recv()
-    got = block(w.z_one)
-    aside.append(w.push(got, got, w.sibling()))
-    yield "copies", [three]
-    three.wait_recv()
-    got = block(w.z_three)
-    aside.append(w.push(got, got, w.sibling()))
-    yield "copies", aside
-    for copy in aside:
-        copy.wait_recv()
+    over = w.push(far, far, w.sibling())
+    yield "copies", [aside, over]
+    aside.wait_recv()
+    over.wait_recv()
+    out, late = stage
+    out[...] = load(mates.there)
+    last = w.push(out, late, w.level_with(w.z_one, [("ze", 2.0)]))
+    yield "copies", [last]
+    last.wait_recv()
+    keep(late[...])
     plan.mark(name)
 
 
@@ -303,7 +309,7 @@
 
 
 def reduce(w, plan, part, scratch, name, after):
-    big, small, mid, far, near, total = scratch
+    big, small, mid, box, near, total = scratch
     over = {}
 
     def half(k, mine, first, second, low):
@@ -319,30 +325,32 @@
         def keep(which, value):
             mid[k, :, :, pl.ds(which * QUARTER, QUARTER)] = value.astype(BF)
 
+        def keep_all(value):
+            mid[k] = value.astype(BF)
+
         def line(i):
             return mid.at[k, i]
 
         def last(value):
             cols = pl.ds(low, HALF)
-            if mine:
-                total[:, cols] = value
-            else:
-                far[:, cols] = value.astype(BF)
-
-        yield from ring_reduce(w, first, sheet, low, [big.at[k, n] for n in range(8)], keep)
+            box[plane, :, cols] = value.astype(BF)
+
+        if DIRECT_REDUCE:
+            bufs = [big.at[k, n] for n in range(3)]
+            yield from ring_total(w, first, lambda i: sheet(i, low, HALF), bufs, keep_all)
+        else:
+            yield from ring_reduce(w, first, sheet, low, [big.at[k, n] for n in range(8)], keep)
         yield from ring_total(w, second, line, [small.at[k, n] for n in range(3)], last)
-        if not mine:
-            cols = pl.ds(low, HALF)
-            over[low] = w.push(far.at[:, cols], near.at[:, cols], w.across())
+        cols = pl.ds(low, HALF)
+        over[k] = w.push(box.at[plane, :, cols], near.at[plane, :, cols], w.across())
         plan.mark(name + "_part")
 
     def finish():
         yield from plan.need((name + "_part", 4))
-        yield "copies", [over[0], over[HALF]]
-        for low in (0, HALF):
-            over[low].wait_recv()
-            cols = pl.ds(low, HALF)
-            total[:, cols] = total[:, cols] + near[:, cols].astype(F32)
+        yield "copies", list(over.values())
+        for copy in over.values():
+            copy.wait_recv()
+        total[...] = box[...].astype(F32) + near[...].astype(F32)
         plan.mark(name)
 
     return [
@@ -356,12 +364,12 @@
 
 def reduce_scratch():
     return [
-        pltpu.VMEM((4, 8, 4, SLOTS, QUARTER), BF),
+        pltpu.VMEM((4, 3, 4, SLOTS, HALF) if DIRECT_REDUCE else (4, 8, 4, SLOTS, QUARTER), BF),
         pltpu.VMEM((4, 3, SLOTS, HALF), BF),
         pltpu.VMEM((4, 4, SLOTS, HALF), BF),
-        pltpu.VMEM((SLOTS, WIDTH), BF),
-        pltpu.VMEM((SLOTS, WIDTH), BF),
-        pltpu.VMEM((SLOTS, WIDTH), F32),
+        pltpu.VMEM((2, SLOTS, WIDTH), BF),
+        pltpu.VMEM((2, SLOTS, WIDTH), BF),
+        pltpu.VMEM((2, SLOTS, WIDTH), F32),
     ]
 
 
@@ -412,6 +420,7 @@
     n1,
     n2,
     dh,
+    dy,
     side,
     n2q,
     dhq,
@@ -419,10 +428,18 @@
     r_dy,
     r_n2,
     r_dh,
-    f_u1,
-    f_a1,
-    f_u2,
-    f_a2,
+    row_stage,
+    row_late,
+    f_u1_near,
+    f_u1_far,
+    f_a1_near,
+    f_a1_far,
+    f_u2_near,
+    f_u2_far,
+    f_a2_near,
+    f_a2_far,
+    stage,
+    late,
     slope1,
     slope2,
     pull2,
@@ -436,7 +453,9 @@
     plan = Plan()
     w = Wires(plan, send, recv)
     me = w.path
-    mate_low, mate_high = partners[0, me], partners[1, me]
+    f_u1, f_a1 = (f_u1_near, f_u1_far), (f_a1_near, f_a1_far)
+    f_u2, f_a2 = (f_u2_near, f_u2_far), (f_a2_near, f_a2_far)
+    mate_low, mate_high = Mates(w, partners, 0), Mates(w, partners, 1)
     scale = 1.0 / jnp.sqrt(jnp.float32(ROWS))
     loads = [
         pltpu.make_async_copy(w_in.at[0], wi, load.at[0]),
@@ -465,19 +484,32 @@
                 packed[p, k] = sorted_rows[2 * p : 2 * p + 2].astype(BF)
 
     w.greet(pack)
-    hops = [w.push(packed.at[to], got.at[me], ({"path": to}, [("z", 0.0)])) for to in w.peers()]
-    got[me] = packed[me]
+    hops, landing = [], got.at[w.zh, me]
+    for to in w.peers():
+        for where in ({"path": to}, {"path": to, **w.across()[0]}):
+            hops.append(w.push(packed.at[to], landing, (where, [("zm", 2.0), ("ze", 2.0)])))
+    hops.append(w.push(packed.at[me], landing, w.across()))
+    got[w.zh, me] = packed[me]
     for copy in hops:
         copy.wait_recv()
-    for p in range(8):
-        x_own[2 * p : 2 * p + 2, :] = got[p, 0].astype(F32)
-        dy_own[2 * p : 2 * p + 2, :] = got[p, 1].astype(F32)
+    for z in range(2):
+        for p in range(8):
+            x_own[z, 2 * p : 2 * p + 2, :] = got[z, p, 0].astype(F32)
+            dy_own[z, 2 * p : 2 * p + 2, :] = got[z, p, 1].astype(F32)
+
+    def spread_rows(full, rows, start=0):
+        for z in range(2):
+            full[z, w.x, w.y, start : start + SLOTS] = rows[z]
+
     rows_n1 = norm_rows(x_own[...], gains[0, 0:1, :]).astype(BF)
-    n1[w.zh, w.x, w.y] = rows_n1
-    r_n1[me] = rows_n1
+    spread_rows(n1, rows_n1)
+    r_n1[w.core] = rows_n1
     rows_dy = dy_own[...].astype(BF)
-    r_dy[me] = rows_dy
-    side[w.zh, w.x, w.y, 0:SLOTS] = rows_dy
+    spread_rows(dy, rows_dy)
+    r_dy[w.core] = rows_dy
+
+    def index(mine):
+        return 0 if mine else 1
 
     def plane_of(mine):
         return w.zh if mine else 1 - w.zh
@@ -490,8 +522,8 @@
 
     def side_rows():
         yield from plan.need(("r_n1", 1), ("r_dy", 1))
-        side[w.zh, w.x, w.y, SLOTS : 2 * SLOTS] = r_n1[mate_low]
-        side[w.zh, w.x, w.y, 2 * SLOTS : 3 * SLOTS] = r_dy[mate_high]
+        spread_rows(side, r_n1[mate_low.here])
+        spread_rows(side, r_dy[mate_high.here], SLOTS)
         plan.mark("side_rows")
 
     def first(mine):
@@ -501,7 +533,7 @@
         value, slope = gelu_both(a)
         u = value.astype(BF)
         slope1[p] = slope
-        f_u1[me, p] = u
+        f_u1[index(mine)][w.core] = u
         for c in range(0, WIDTH, QUARTER):
             y = dot(u, wo[0, :, c : c + QUARTER]).astype(BF)
             part1[p, :, :, :, c : c + QUARTER] = y.reshape(4, 4, SLOTS, QUARTER)
@@ -513,15 +545,15 @@
         yield from plan.need(("red1", 1))
         h = (x_own[...] + red1[5][...]).astype(BF).astype(F32)
         rows = norm_rows(h, gains[0, 1:2, :]).astype(BF)
-        n2[w.zh, w.x, w.y] = rows
-        r_n2[me] = rows
+        spread_rows(n2, rows)
+        r_n2[w.core] = rows
         plan.work(0.6)
         plan.mark("n2_own")
 
     def pull(mine):
         p = plane_of(mine)
-        yield from plan.need((("side", mine), 2), ("weights", 1))
-        pull2[p] = dot_t(side[p, :, :, 0:SLOTS, :].reshape(PLANE, WIDTH), wo[1])
+        yield from plan.need((("dy", mine), 2), ("weights", 1))
+        pull2[p] = dot_t(dy[p].reshape(PLANE, WIDTH), wo[1])
         plan.work(0.8)
         plan.mark(("pull2", mine))
 
@@ -530,9 +562,9 @@
         yield from plan.need((("n2", mine), 2), (("pull2", mine), 1))
         a = dot(n2[p].reshape(PLANE, WIDTH), wi[1])
         value, slope = gelu_both(a)
-        f_u2[me, p] = value.astype(BF)
+        f_u2[index(mine)][w.core] = value.astype(BF)
         da = (pull2[p] * slope).astype(BF)
-        f_a2[me, p] = da
+        f_a2[index(mine)][w.core] = da
         for c in range(0, WIDTH, QUARTER):
             y = dot_t(da, wi[1, c : c + QUARTER, :]).astype(BF)
             part2[p, :, :, :, c : c + QUARTER] = y.reshape(4, 4, SLOTS, QUARTER)
@@ -542,7 +574,7 @@
 
     def side_n2():
         yield from plan.need(("r_n2", 1))
-        n2q[w.zh, w.x, w.y] = r_n2[mate_high]
+        spread_rows(n2q, r_n2[mate_high.here])
         plan.mark("n2q_own")
 
     def back():
@@ -550,23 +582,29 @@
         h = (x_own[...] + red1[5][...]).astype(BF).astype(F32)
         grad = norm_pull(h, gains[0, 1:2, :], red2[5][...])
         rows = (dy_own[...] + grad).astype(BF)
-        dh[w.zh, w.x, w.y] = rows
-        r_dh[me] = rows
+        spread_rows(dh, rows)
+        r_dh[w.core] = rows
         plan.work(0.8)
         plan.mark("dh_own")
 
     def side_dh():
         yield from plan.need(("r_dh", 1))
-        dhq[w.zh, w.x, w.y] = r_dh[mate_low]
+        spread_rows(dhq, r_dh[mate_low.here])
         plan.mark("dhq_own")
 
     def third(mine):
         p = plane_of(mine)
         yield from plan.need((("dh", mine), 2))
         du = dot_t(dh[p].reshape(PLANE, WIDTH), wo[0])
-        f_a1[me, p] = (du * slope1[p]).astype(BF)
+        f_a1[index(mine)][w.core] = (du * slope1[p]).astype(BF)
         plan.work(0.8)
         plan.mark(("a1", mine))
+
+    def in_order(factor, k):
+        near, far = factor[0][k], factor[1][k]
+        swap = w.zh == 1
+        top, bottom = jnp.where(swap, far, near), jnp.where(swap, near, far)
+        return jnp.concatenate([top, bottom], axis=0).T
 
     def delta(out, level, k, own, mate, own_rows, mate_rows, own_needs, mate_needs, turned):
         def product(factor, rows, cols):
@@ -574,17 +612,17 @@
 
         def first_part():
             yield from plan.need(*own_needs)
-            factor = own[me].reshape(ROWS, HIDDEN).T
+            factor = in_order(own, w.core)
             for c in range(0, WIDTH, QUARTER):
                 cols = slice(c, c + QUARTER)
                 own_part[k, :, cols] = product(factor, own_rows, cols)
-                plan.work(0.5)
+                plan.work(0.15)
                 yield from plan.need()
             plan.mark(("delta", k))
 
         def second_part():
             yield from plan.need((("delta", k), 1), *mate_needs)
-            factor = own[mate].reshape(ROWS, HIDDEN).T
+            factor = in_order(own, mate.here)
             for c in range(0, WIDTH, QUARTER):
                 cols = slice(c, c + QUARTER)
                 there = product(factor, mate_rows, cols).astype(F32)
@@ -593,7 +631,7 @@
                     out[level, cols, :] = mean.T
                 else:
                     out[level, :, cols] = mean
-                plan.work(0.6)
+                plan.work(0.22)
                 yield from plan.need()
 
         return [first_part(), second_part()]
@@ -607,62 +645,90 @@
     def both(name):
         return [((name, True), 2), ((name, False), 2)]
 
-    def spread(f, name, after):
-        return [
-            path_gather(
+    def spread(f, number, mates, name, after):
+        for mine in (True, False):
+            i = index(mine)
+
+            def keep(value, i=i):
+                f[i][4] = value
+
+            yield path_fetch(
                 w,
                 plan,
-                lambda q, p=plane_of(mine): f.at[q, p],
+                lambda k, i=i: f[i].at[k],
+                lambda k, i=i: f[i][k],
+                keep,
+                (stage.at[number, i], late.at[number, i]),
+                mates,
                 name,
                 [((after, mine), 1)],
             )
-            for mine in (True, False)
-        ]
-
-    main = [load_weights()]
-    main += gather(w, plan, n1, "n1", [])
-    main += [first(True), first(False)]
-    main += reduce(w, plan, part1, red1, "red1", "part1")
-    main += [middle()]
-    main += gather(w, plan, n2, "n2", [("n2_own", 1)])
-    main += [second(True), second(False)]
-    main += reduce(w, plan, part2, red2, "red2", "part2")
-    main += [back()]
-    main += gather(w, plan, dh, "dh", [("dh_own", 1)])
-    main += [third(True), third(False)]
-    tail = [path_gather(w, plan, lambda q: r_dh.at[q], "r_dh", [("dh_own", 1)]), side_dh()]
-    tail += gather(w, plan, dhq, "dhq", [("dhq_own", 1)])
-    tail += spread(f_a1, "f_a1", "a1")
-    low = [path_gather(w, plan, lambda q: r_dy.at[q], "r_dy", [])]
-    low += [path_gather(w, plan, lambda q: r_n1.at[q], "r_n1", [])]
-    low += [side_rows()]
-    low += gather(w, plan, side, "side", [("side_rows", 1)])
-    low += [pull(True), pull(False)]
-    low += spread(f_u1, "f_u1", "part1")
-    low += [path_gather(w, plan, lambda q: r_n2.at[q], "r_n2", [("n2_own", 1)]), side_n2()]
-    low += spread(f_u2, "f_u2", "part2")
-    low += spread(f_a2, "f_a2", "part2")
-    low += gather(w, plan, n2q, "n2q", [("n2q_own", 1)])
+
+    def rows_over(ref, number, mates, name, after):
+        def keep(value):
+            ref[4] = value
+
+        return path_fetch(
+            w,
+            plan,
+            lambda k: ref.at[k],
+            lambda k: ref[k],
+            keep,
+            (row_stage.at[number], row_late.at[number]),
+            mates,
+            name,
+            after,
+        )
+
+    def parts(name):
+        return [((name, True), 1), ((name, False), 1)]
 
     high_out = delta(
-        d_out, 1, 0, f_u2, mate_high, of_side(0), of_side(2),
-        both("side") + [(("part2", True), 1), (("part2", False), 1)], [("f_u2", 2)], False,
+        d_out, 1, 0, f_u2, mate_high, of(dy), of_side(1),
+        both("dy") + parts("part2"), [("f_u2", 2)] + both("side"), False,
     )
     high_in = delta(
         d_in, 1, 1, f_a2, mate_high, of(n2), of(n2q),
-        both("n2") + [(("part2", True), 1), (("part2", False), 1)], [("f_a2", 2)] + both("n2q"), True,
+        both("n2") + parts("part2"), [("f_a2", 2)] + both("n2q"), True,
     )
     low_out = delta(
         d_out, 0, 2, f_u1, mate_low, of(dh), of(dhq),
         both("dh"), [("f_u1", 2)] + both("dhq"), False,
     )
     low_in = delta(
-        d_in, 0, 3, f_a1, mate_low, of(n1), of_side(1),
-        [(("a1", True), 1), (("a1", False), 1)], [("f_a1", 2)] + both("side"), True,
+        d_in, 0, 3, f_a1, mate_low, of(n1), of_side(0),
+        parts("a1"), [("f_a1", 2)] + both("side"), True,
     )
-    low += high_out + high_in
-    tail += low_out + low_in
-    plan.run([(0.0, t) for t in main] + [(0.5, t) for t in tail] + [(SIDE_LAG, t) for t in low])
+    groups = [
+        ("load", [load_weights()]),
+        ("n1", gather(w, plan, n1, "n1", [])),
+        ("first", [first(True), first(False)]),
+        ("red1", reduce(w, plan, part1, red1, "red1", "part1")),
+        ("mid", [middle()]),
+        ("n2", gather(w, plan, n2, "n2", [("n2_own", 1)])),
+        ("second", [second(True), second(False)]),
+        ("red2", reduce(w, plan, part2, red2, "red2", "part2")),
+        ("back", [back()]),
+        ("dh", gather(w, plan, dh, "dh", [("dh_own", 1)])),
+        ("third", [third(True), third(False)]),
+        ("r_dh", [rows_over(r_dh, 3, mate_low, "r_dh", [("dh_own", 1)]), side_dh()]),
+        ("dhq", gather(w, plan, dhq, "dhq", [("dhq_own", 1)])),
+        ("f_a1", spread(f_a1, 1, mate_low, "f_a1", "a1")),
+        ("own", [low_out[0], low_in[0]]),
+        ("end", [low_out[1], low_in[1]]),
+        ("dy", gather(w, plan, dy, "dy", [])),
+        ("pull", [pull(True), pull(False)]),
+        ("r_dy", [rows_over(r_dy, 1, mate_high, "r_dy", [])]),
+        ("r_n1", [rows_over(r_n1, 0, mate_low, "r_n1", []), side_rows()]),
+        ("side", gather(w, plan, side, "side", [("side_rows", 1)])),
+        ("f_u1", spread(f_u1, 0, mate_low, "f_u1", "part1")),
+        ("r_n2", [rows_over(r_n2, 2, mate_high, "r_n2", [("n2_own", 1)]), side_n2()]),
+        ("f_u2", spread(f_u2, 2, mate_high, "f_u2", "part2")),
+        ("f_a2", spread(f_a2, 3, mate_high, "f_a2", "part2")),
+        ("n2q", gather(w, plan, n2q, "n2q", [("n2q_own", 1)])),
+        ("high", high_out + high_in),
+    ]
+    plan.run([LAGS.get(name, (0.0, 0.0)) + (t,) for name, tasks in groups for t in tasks])
     w.drain()
 
 
@@ -674,10 +740,10 @@
         return pltpu.VMEM((2, 4, 4, rows, WIDTH), BF)
 
     def by_path():
-        return pltpu.VMEM((8, SLOTS, WIDTH), BF)
+        return pltpu.VMEM((5, 2, SLOTS, WIDTH), BF)
 
     def factor():
-        return pltpu.VMEM((8, 2, PLANE, HIDDEN), BF)
+        return pltpu.VMEM((5, PLANE, HIDDEN), BF)
 
     return pl.pallas_call(
         step_kernel,
@@ -689,25 +755,34 @@
         out_specs=[vmem, vmem],
         scratch_shapes=[
             pltpu.VMEM((8, 2, 2, WIDTH), BF),
-            pltpu.VMEM((8, 2, 2, WIDTH), BF),
-            pltpu.VMEM((SLOTS, WIDTH), F32),
-            pltpu.VMEM((SLOTS, WIDTH), F32),
+            pltpu.VMEM((2, 8, 2, 2, WIDTH), BF),
+            pltpu.VMEM((2, SLOTS, WIDTH), F32),
+            pltpu.VMEM((2, SLOTS, WIDTH), F32),
             pltpu.VMEM((2, WIDTH, HIDDEN), BF),
             pltpu.VMEM((2, HIDDEN, WIDTH), BF),
             full(SLOTS),
             full(SLOTS),
             full(SLOTS),
-            full(3 * SLOTS),
+            full(SLOTS),
+            full(2 * SLOTS),
             full(SLOTS),
             full(SLOTS),
             by_path(),
             by_path(),
             by_path(),
             by_path(),
+            pltpu.VMEM((4, 2, SLOTS, WIDTH), BF),
+            pltpu.VMEM((4, 2, SLOTS, WIDTH), BF),
             factor(),
             factor(),
             factor(),
             factor(),
+            factor(),
+            factor(),
+            factor(),
+            factor(),
+            pltpu.VMEM((4, 2, PLANE, HIDDEN), BF),
+            pltpu.VMEM((4, 2, PLANE, HIDDEN), BF),
             pltpu.VMEM((2, PLANE, HIDDEN), F32),
             pltpu.VMEM((2, PLANE, HIDDEN), F32),
             pltpu.VMEM((2, PLANE, HIDDEN), F32),

time: 187 us -> 159 us (0.85)
  Pallas kernels: 180 us -> 151 us
    pallas_call x1, Pallas kernels: 180 us -> 151 us  [step_call(): pl.pallas_call(step_kernel, out_shape=[jax.ShapeDtypeStruct((2, WIDTH, HI...]
where the time goes in v3:
time: 159 us; the launch traced here: 157 us
  Pallas kernels  151 us (95%)
  local copies, waits for them, and re-layouts  5.85 us (4%)
    pallas_call x1, Pallas kernels, step_call(): pl.pallas_call(step_kernel, out_shape=[jax.ShapeDtypeStruct((2, WIDTH, HI...  151 us
    unnamed x5, local copies, waits for them, and re-layouts  5.85 us

profile of v3, /device:TPU:1, one launch (start us, length us, event | category | flops | bytes accessed | tf_op | source)
XLA Modules:
  0.0 157.2 jit_solution(13523370235994633368)
XLA Ops:
  0.6 1.3 copy.9.routes
  2.0 150.7 %shard_map.86 = (bf16[2,2048,256]{2,1,0:T(8,128)(2,1)}, bf16[2,256,2048]{2,1,0:T(8,128)(2,1)}) custom-call(s32[2,8]{1,0:T(2,128)} %partners.1, bf16[12,2048]{1,0:T(8,128)(2,1)} %tokens.1, s32[12,1]{1,0:T(8,128)} %copy.9.routes, bf16[12,2048]{1,0:T(8,128)(2,1)} %cotangent.1, bf16[1,2,2048]{2,1,0:T(2,128)(2,1)} %gains.1, bf16[1,2,2048,256]{3,2,1,0:T(8,128)(2,1)} %w_in.1, ...), custom_call_target="tpu_custom_call" | custom-call | tf_op jit(solution)/shard_map/pallas_call | solution.py:748
  152.7 0.0 copy-start
  152.7 3.2 %copy.12 = bf16[1,2,2048,256]{3,2,1,0:T(8,128)(2,1)} copy(bf16[1,2,2048,256]{3,2,1,0:T(8,128)(2,1)} %bitcast.3) | data formatting | bytes 4194304
  155.9 0.0 copy-done
  155.9 1.3 copy.13
Async XLA Ops:
  152.7 3.2 %copy-start = (bf16[2,256,2048]{2,1,0:T(8,128)(2,1)S(1)}, bf16[2,256,2048]{2,1,0:T(8,128)(2,1)}, u32[]{:S(2)}) copy-start(bf16[2,256,2048]{2,1,0:T(8,128)(2,1)} %get-tuple-element.5) | copy-start | bytes 6291460

commit v4 on v3

--- a/solution.py
+++ b/solution.py
@@ -16,7 +16,7 @@
 ROWS = 512
 PLANE = 256
 COPIES = 480
-RATE = 90000.0
+RATE = 82000.0
 DELAY = 2.5
 DIRECT_REDUCE = False
 STRAIGHT = {'n2': (True, False), 'n2q': (True, False), 'dh': (False, False), 'n1': (True, False), 'dy': (False, False), 'side': (False, False), 'dhq': (True, False)}

time: 159 us -> 158 us (level)
  no operation moved by 1% of the time
where the time goes in v4:
time: 158 us; the launch traced here: 157 us
  Pallas kernels  151 us (96%)
  local copies, waits for them, and re-layouts  5.85 us (4%)
    pallas_call x1, Pallas kernels, step_call(): pl.pallas_call(step_kernel, out_shape=[jax.ShapeDtypeStruct((2, WIDTH, HI...  151 us
    unnamed x5, local copies, waits for them, and re-layouts  5.85 us

profile of v4, /device:TPU:1, one launch (start us, length us, event | category | flops | bytes accessed | tf_op | source)
XLA Modules:
  0.0 157.3 jit_solution(8442751370192542201)
XLA Ops:
  0.6 1.3 copy.9.routes
  2.0 150.8 %shard_map.86 = (bf16[2,2048,256]{2,1,0:T(8,128)(2,1)}, bf16[2,256,2048]{2,1,0:T(8,128)(2,1)}) custom-call(s32[2,8]{1,0:T(2,128)} %partners.1, bf16[12,2048]{1,0:T(8,128)(2,1)} %tokens.1, s32[12,1]{1,0:T(8,128)} %copy.9.routes, bf16[12,2048]{1,0:T(8,128)(2,1)} %cotangent.1, bf16[1,2,2048]{2,1,0:T(2,128)(2,1)} %gains.1, bf16[1,2,2048,256]{3,2,1,0:T(8,128)(2,1)} %w_in.1, ...), custom_call_target="tpu_custom_call" | custom-call | tf_op jit(solution)/shard_map/pallas_call | solution.py:748
  152.7 0.0 copy-start
  152.7 3.2 %copy.12 = bf16[1,2,2048,256]{3,2,1,0:T(8,128)(2,1)} copy(bf16[1,2,2048,256]{3,2,1,0:T(8,128)(2,1)} %bitcast.3) | data formatting | bytes 4194304
  155.9 0.0 copy-done
  155.9 1.3 copy.13
Async XLA Ops:
  152.7 3.2 %copy-start = (bf16[2,256,2048]{2,1,0:T(8,128)(2,1)S(1)}, bf16[2,256,2048]{2,1,0:T(8,128)(2,1)}, u32[]{:S(2)}) copy-start(bf16[2,256,2048]{2,1,0:T(8,128)(2,1)} %get-tuple-element.5) | copy-start | bytes 6291460
